TPU v7x, 512 devices: a whole 4x8x8 slice. The times are simulated.
512 devices in a mesh: replica: 16 (over y_lo, z), fsdp: 32 (over y_hi, x, core).
Axes of the slice: x: 4, y: 8 (y_hi: 4, y_lo: 2; y = y_hi * 2 + y_lo), z: 8, core: 2. Of those that a mesh axis runs over, the one named last changes fastest.
Arguments:
- node_feats: bfloat16 [65536, 1024], P(('replica', 'fsdp')), may hold values from -6 to 6
- neighbor_src: int32 [12, 65536], P(None, ('replica', 'fsdp')), may hold values from 0 to 4095, as said below
- distances: float32 [12, 65536], P(None, ('replica', 'fsdp')), may hold values from 0.8 to 5
- graph_ids: int32 [16, 4096], P('replica', 'fsdp'), may hold values from 0 to 7, never falling along the last dimension, each value on 1 to 1024 neighbouring positions
- msg_weight: bfloat16 [1024, 1024], P('fsdp'), may hold values from -0.1875 to 0.1875
- out_weight: bfloat16 [1024, 1024], P('fsdp'), may hold values from -0.1875 to 0.1875
- radial_weight: float32 [8, 1024], replicated, may hold values from -6 to 6
- cotangent: bfloat16 [65536, 1024], P(('replica', 'fsdp')), may hold values from -6 to 6
- fragment: int32 [1], replicated, may hold values from 0 to 7
Outputs:
- node_out: bfloat16 [65536, 1024], P(('replica', 'fsdp'))
- grad_msg: bfloat16 [16, 1024, 1024], P('replica', 'fsdp')
- grad_out: bfloat16 [16, 1024, 1024], P('replica', 'fsdp')
- outer_sum: float32 [2, 1024, 128], P(None, 'fsdp')
Inputs may be any that keep to these rules, and one draw needn't show every extreme that they name: `neighbor_src`: each neighbour index lies within 32 positions of its own atom's index in the group, never equal to it, and inside the group. `graph_ids`: within each group the graph numbers never fall and every graph has at least one atom.
All inputs are finite; a program needn't handle non-finite values. Where the computation divides by a largest or mean magnitude, that divisor is 1e-20 or more.
Results may differ from a plain program's by a relative error of at most 0.02.
Values may be sent and summed in bfloat16 or wider, within the bound.
A program may use at most 64 MiB of HBM per device.

v0:
```python
import math

import jax
import jax.numpy as jnp
from jax import lax
from jax.sharding import PartitionSpec as P

FRAG = 128
GRAPHS = 8


cutoff = 5.0
sharpness = 2.0
tiny = 1e-06


def with_halo(cells, sides, width):
    for axis, dim in sides:
        count = lax.axis_size(axis)
        ends = count - 1
        head = lax.slice_in_dim(cells, 0, width, axis=dim)
        tail = lax.slice_in_dim(cells, cells.shape[dim] - width, cells.shape[dim], axis=dim)
        cells = jnp.concatenate(
            [
                lax.ppermute(tail, axis, [(i, (i + 1) % count) for i in range(ends)]),
                cells,
                lax.ppermute(head, axis, [((i + 1) % count, i) for i in range(ends)]),
            ],
            axis=dim,
        )
    return cells


def passed_along(value, axis, steps):
    count = lax.axis_size(axis)
    leading, last = (max(0, -steps), min(count, count - steps))
    return lax.ppermute(value, axis, [(source, source + steps) for source in range(leading, last)])


def radial(dist_row, radial_weight):
    basis_count = radial_weight.shape[0]
    centers = cutoff * jnp.arange(basis_count).astype(jnp.float32) / (basis_count - 1)
    envelope = 0.5 * (jnp.cos(jnp.pi * dist_row / cutoff) + 1.0)
    basis = jnp.exp(-sharpness * (dist_row[:, None] - centers[None, :]) ** 2) * envelope[:, None]
    return jnp.dot(
        basis, radial_weight, precision=lax.Precision.HIGHEST, preferred_element_type=jnp.float32
    )


def contract_rows(left, right):
    return lax.dot_general(
        left, right, (((0,), (0,)), ((), ())), preferred_element_type=jnp.float32
    )


def shards(
    node_feats,
    neighbor_src,
    distances,
    graph_ids,
    msg_weight,
    out_weight,
    radial_weight,
    cotangent,
    fragment,
):
    atoms = node_feats.shape[0]
    width = node_feats.shape[1]
    neighbors = neighbor_src.shape[0]
    margin = atoms // 4
    norm = 1.0 / math.sqrt(neighbors)
    first_atom = lax.axis_index("fsdp") * atoms
    empty = jnp.zeros((atoms, width), jnp.float32)
    inputs = node_feats
    projected = jnp.dot(
        inputs,
        lax.all_gather(msg_weight, "fsdp", axis=0, tiled=True),
        preferred_element_type=jnp.float32,
    ).astype(jnp.bfloat16)
    extended = with_halo(projected, (("fsdp", 0),), margin)
    local_src = neighbor_src - first_atom + margin

    def gather_step(k, acc):
        rows = jnp.take(extended, local_src[k], axis=0).astype(jnp.float32)
        return acc + radial(distances[k], radial_weight) * rows

    agg = lax.fori_loop(0, neighbors, gather_step, empty) * norm
    act = jax.nn.silu(agg).astype(jnp.bfloat16)
    inputs = act
    branch_sum = jnp.dot(
        inputs,
        lax.all_gather(out_weight, "fsdp", axis=0, tiled=True),
        preferred_element_type=jnp.float32,
    )
    node_out = (node_feats.astype(jnp.float32) + branch_sum).astype(jnp.bfloat16)
    ids = graph_ids[0]
    onehot = (ids[:, None] == jnp.arange(GRAPHS, dtype=jnp.int32)[None, :]).astype(jnp.float32)
    own_counts = jnp.sum(onehot, axis=0).astype(jnp.int32)
    counts = lax.psum(own_counts, "fsdp")
    weight = jnp.sum(onehot * lax.rsqrt(counts.astype(jnp.float32))[None, :], axis=1)
    dout = (weight[:, None] * cotangent.astype(jnp.float32)).astype(jnp.bfloat16)
    out_rows = lax.psum_scatter(
        contract_rows(act, dout).astype(jnp.bfloat16), "fsdp", scatter_dimension=0, tiled=True
    ).astype(jnp.float32)
    dact = lax.dot_general(
        dout,
        lax.all_gather(out_weight, "fsdp", axis=0, tiled=True),
        (((1,), (1,)), ((), ())),
        preferred_element_type=jnp.float32,
    )
    sig = jax.nn.sigmoid(agg)
    dagg = dact * sig * (1.0 + agg * (1.0 - sig))

    def spread_step(k, acc):
        return acc.at[local_src[k]].add(radial(distances[k], radial_weight) * dagg * norm)

    spread = lax.fori_loop(
        0, neighbors, spread_step, jnp.zeros((atoms + 2 * margin, width), jnp.float32)
    )
    lower_rim = spread[:margin]
    upper_rim = spread[margin + atoms :]
    from_below = passed_along(upper_rim.astype(jnp.bfloat16), "fsdp", 1).astype(upper_rim.dtype)
    from_above = passed_along(lower_rim.astype(jnp.bfloat16), "fsdp", -1).astype(lower_rim.dtype)
    dproj = spread[margin : margin + atoms]
    dproj = dproj.at[:margin].add(from_below)
    dproj = dproj.at[atoms - margin :].add(from_above)
    dproj = dproj.astype(jnp.bfloat16)
    msg_rows = lax.psum_scatter(
        contract_rows(node_feats, dproj).astype(jnp.bfloat16),
        "fsdp",
        scatter_dimension=0,
        tiled=True,
    ).astype(jnp.float32)
    column = fragment[0] * FRAG
    pieces = jnp.stack(
        [
            lax.dynamic_slice_in_dim(msg_rows, column, FRAG, 1),
            lax.dynamic_slice_in_dim(out_rows, column, FRAG, 1),
        ]
    )
    scale = (jnp.max(jnp.abs(pieces), axis=-1, keepdims=True) + tiny).astype(jnp.bfloat16)
    code = (pieces / scale.astype(jnp.float32)).astype(jnp.bfloat16)
    outer_sum = lax.psum(
        (scale.astype(jnp.float32) * code.astype(jnp.float32)).astype(jnp.bfloat16), "replica"
    ).astype(jnp.float32)
    return (
        node_out,
        msg_rows.astype(jnp.bfloat16)[None],
        out_rows.astype(jnp.bfloat16)[None],
        outer_sum,
    )


def solution(mesh):
    placed = (
        P(("replica", "fsdp"), None),
        P(None, ("replica", "fsdp")),
        P(None, ("replica", "fsdp")),
        P("replica", "fsdp"),
        P("fsdp", None),
        P("fsdp", None),
        P(),
        P(("replica", "fsdp"), None),
        P(),
    )
    return jax.shard_map(
        shards,
        mesh=mesh,
        in_specs=placed,
        out_specs=(
            P(("replica", "fsdp"), None),
            P("replica", "fsdp", None),
            P("replica", "fsdp", None),
            P(None, "fsdp", None),
        ),
        check_vma=False,
    )
```

profile of v0, /device:TPU:8, one launch (start us, length us, event | category | flops | bytes accessed | tf_op | source)
XLA Modules:
  0.0 413.5 jit_solution(17825532584873003960)
XLA Ops:
  9.5 18.2 %psum.14 = s32[8]{0:T(128)S(1)} all-reduce(s32[8]{0:T(128)S(1)} %convert_element_type.127), channel_id=1, replica_groups=mesh['replica'=16,'fsdp'=32] {'fsdp'}, use_global_device_ids=true, to_apply=%region_3.4 | all-reduce | flops 8 | bytes 64 | tf_op jit(solution)/shard_map/psum | solution.py:99
  28.4 45.7 %all-gather.3.cloned.1.call-done = bf16[1024,1024]{1,0:T(8,128)(2,1)} async-done(((bf16[32,1024]{1,0:T(8,128)(2,1)}), bf16[1024,1024]{1,0:T(8,128)(2,1)}) %all-gather.3.cloned.1.call-update) | async-done | bytes 2097168 | tf_op jit(solution)/shard_map/all_gather | solution.py:77
  74.1 2.1 convolution_convert_fusion.1
  76.2 2.1 collective-permute-start
  78.4 1.3 collective-permute-start.1
  79.8 2.2 collective-permute-done.1
  82.0 29.7 %while.34 = (s32[]{:T(128)}, f32[128,1024]{1,0:T(8,128)S(1)}, f32[12,128]{1,0:T(8,128)}, f32[8,1024]{1,0:T(8,128)S(1)}, s32[12,128]{1,0:T(8,128)S(1)}, /*index=5*/bf16[192,1024]{1,0:T(8,128)(2,1)S(1)}, s32[]{:T(128)}, s32[]{:T(128)}) while((s32[]{:T(128)}, f32[128,1024]{1,0:T(8,128)S(1)}, f32[12,128]{1,0:T(8,128)}, ...), condition=%wide.region_1.0_spmd.clone, body=%wide.region_0.1_spmd.clone.sunk | while | flops 13244947 | bytes 1877427 | solution.py:87
  111.7 2.1 convolution_convert_fusion
  113.9 20.3 %all-gather.5.cloned.1.call-done = bf16[1024,1024]{1,0:T(8,128)(2,1)} async-done(((bf16[32,1024]{1,0:T(8,128)(2,1)}), bf16[1024,1024]{1,0:T(8,128)(2,1)}) %all-gather.5.cloned.1.call-update) | async-done | bytes 2097168 | tf_op jit(solution)/shard_map/all_gather | solution.py:92
  134.2 2.5 fusion.24
  136.7 41.1 %while.33 = (s32[]{:T(128)}, f32[192,1024]{1,0:T(8,128)S(1)}, s32[12,128]{1,0:T(8,128)S(1)}, f32[12,128]{1,0:T(8,128)}, f32[8,1024]{1,0:T(8,128)S(1)}, /*index=5*/f32[128,1024]{1,0:T(8,128)S(1)}, s32[]{:T(128)}) while((s32[]{:T(128)}, f32[192,1024]{1,0:T(8,128)S(1)}, s32[12,128]{1,0:T(8,128)S(1)}, f32[12,128]{1,0:T(8,128)}, ...), condition=%wide.region_7.8_spmd, body=%wide.region_5.7_spmd.sunk | while | flops 12981010 | bytes 2658461 | solution.py:117
  138.2 1.9 scatter_fusion
  141.6 1.9 scatter_fusion
  145.0 1.9 scatter_fusion
  148.5 1.9 scatter_fusion
  151.9 1.9 scatter_fusion
  155.3 1.9 scatter_fusion
  158.7 1.9 scatter_fusion
  162.2 1.9 scatter_fusion
  165.6 1.9 scatter_fusion
  169.0 1.9 scatter_fusion
  172.4 1.9 scatter_fusion
  175.9 1.9 scatter_fusion
  177.9 2.1 collective-permute-start.2
  180.1 1.3 collective-permute-start.3
  181.4 2.1 collective-permute-done.3
  184.3 2.6 copy.22
  188.5 1.2 fusion.25
  189.7 47.1 %reduce-scatter.5.cloned.1.call-done = bf16[32,1024]{1,0:T(8,128)(2,1)} async-done(((bf16[1024,1024]{1,0:T(8,128)(2,1)}), bf16[32,1024]{1,0:T(8,128)(2,1)}) %reduce-scatter.5.cloned.1.call-update) | async-done | bytes 65552 | tf_op jit(solution)/shard_map/reduce_scatter | solution.py:102
  237.5 101.5 %reduce-scatter.7.cloned.1.call-done = bf16[32,1024]{1,0:T(8,128)(2,1)} async-done(((bf16[1024,1024]{1,0:T(8,128)(2,1)}), bf16[32,1024]{1,0:T(8,128)(2,1)}) %reduce-scatter.7.cloned.1.call-update) | async-done | bytes 65552 | tf_op jit(solution)/shard_map/reduce_scatter | solution.py:128
  339.9 64.7 %psum.15 = bf16[2,32,128]{2,1,0:T(8,128)(2,1)S(1)} all-reduce(bf16[2,32,128]{2,1,0:T(8,128)(2,1)S(1)} %multiply_convert_fusion.4), channel_id=1, replica_groups=mesh['replica'=16,'fsdp'=32] {'replica'}, use_global_device_ids=true, to_apply=%region_11.12 | all-reduce | flops 8192 | bytes 32768 | tf_op jit(solution)/shard_map/psum | solution.py:143
  405.2 1.0 copy.23
  (174 shorter events, 54.5 us)
Async XLA Ops:
  7.2 72.5 %copy-start.4 = (s32[1,128]{1,0:T(1,128)S(1)}, s32[1,128]{1,0:T(1,128)}, u32[]{:S(2)}) copy-start(s32[1,128]{1,0:T(1,128)} %param.20) | copy-start | bytes 1540
  7.2 74.8 %copy-start = (f32[8,1024]{1,0:T(8,128)S(1)}, f32[8,1024]{1,0:T(8,128)}, u32[]{:S(2)}) copy-start(f32[8,1024]{1,0:T(8,128)} %param.23) | copy-start | bytes 98308
  7.2 66.9 %all-gather.3.cloned.1.call-start = ((), (), s32[]{:S(2)}) async-start(), calls=%async_computation.2 | async-start | bytes 2162688 | tf_op jit(solution)/shard_map/all_gather | solution.py:77
  7.9 126.2 %all-gather.5.cloned.1.call-start = ((), (), s32[]{:S(2)}) async-start(), calls=%async_computation.3 | async-start | bytes 2162688 | tf_op jit(solution)/shard_map/all_gather | solution.py:92
  8.7 228.1 %reduce-scatter.5.cloned.1.call-start = ((), (), s32[]{:S(2)}) async-start(), calls=%async_computation.4 | async-start | bytes 2162688 | tf_op jit(solution)/shard_map/reduce_scatter | solution.py:102
  76.2 3.5 collective-permute-start
  78.4 3.6 collective-permute-start.1
  82.0 29.7 %copy-start.3 = (bf16[128,1024]{1,0:T(8,128)(2,1)S(1)}, bf16[128,1024]{1,0:T(8,128)(2,1)}, u32[]{:S(2)}) copy-start(bf16[128,1024]{1,0:T(8,128)(2,1)} %param.24) | copy-start | bytes 786436
  113.8 225.2 %reduce-scatter.7.cloned.1.call-start = ((), (), s32[]{:S(2)}) async-start(), calls=%async_computation.5 | async-start | bytes 2162688 | tf_op jit(solution)/shard_map/reduce_scatter | solution.py:128
  177.8 5.8 %copy-start.1 = (bf16[128,1024]{1,0:T(8,128)(2,1)S(1)}, bf16[128,1024]{1,0:T(8,128)(2,1)}, u32[]{:S(2)}) copy-start(bf16[128,1024]{1,0:T(8,128)(2,1)} %param.17) | copy-start | bytes 786436
  177.9 3.5 collective-permute-start.2
  180.1 3.5 collective-permute-start.3
  186.9 1.6 copy-start.2
Sparse Core Ops, SparseCore 0:
  11.1 62.8 all-gather.2
  77.2 56.9 all-gather.4
  139.1 97.5 reduce-scatter.4
  241.0 97.8 reduce-scatter.6
where the time goes:
time: 415 us; the launch traced here: 413 us
  waiting for transfers between devices  220 us (53%)
  blocking collectives  82.8 us (20%)
  other arithmetic  45.4 us (11%)
  matrix products  26.5 us (6%)
  local copies, waits for them, and re-layouts  15.6 us (4%)
  between operations  14.8 us (4%)
  starting transfers between devices  6.99 us (2%)
    reduce_scatter x1, waiting for transfers between devices, shards(): lax.psum_scatter(contract_rows(node_feats, dproj).astype(jnp.bfloat16), '...  102 us
    psum x1, blocking collectives, shards(): lax.psum((scale.astype(jnp.float32) * code.astype(jnp.float32)).astype(jn...  64.7 us
    reduce_scatter x1, waiting for transfers between devices, shards(): lax.psum_scatter(contract_rows(act, dout).astype(jnp.bfloat16), 'fsdp', s...  47.1 us
    all_gather x1, waiting for transfers between devices, shards(): lax.all_gather(msg_weight, 'fsdp', axis=0, tiled=True)  45.7 us
    scatter-add x12, other arithmetic, spread_step(): acc.at[local_src[k]].add(radial(distances[k], radial_weight) * dagg * norm)  23.1 us
    all_gather x1, waiting for transfers between devices, shards(): lax.all_gather(out_weight, 'fsdp', axis=0, tiled=True)  20.3 us
    psum x1, blocking collectives, shards(): counts = lax.psum(own_counts, 'fsdp')  18.2 us
    dot_general x24, matrix products, radial(): jnp.dot(basis, radial_weight, precision=lax.Precision.HIGHEST, preferred_...  17.9 us
  transfers between devices with their start and end apart: 8, of which 6 were waited for; matrix products, arithmetic and copies ran while one was open for 20% of the time, Pallas kernels for 0%

commit v1 on v0

v1 whole, which is shorter than its diff:
```python
import functools
import math

import jax
import jax.numpy as jnp
from jax import lax
from jax.experimental import pallas as pl
from jax.experimental.pallas import tpu as pltpu
from jax.sharding import PartitionSpec as P

MESH = pl.DeviceIdType.MESH
F32 = jnp.float32
BF16 = jnp.bfloat16
GRAPHS = 8
FRAG = 128
A = 128
C = 1024
HC = 512
H = 32
NB = 12
BASIS = 8
W = 2 * A - 64
EXT = 2 * A + 2 * H
TINY = 1e-6


def contract(a, b, da, db):
    return lax.dot_general(a, b, (((da,), (db,)), ((), ())), preferred_element_type=F32)


def body(
    feats, src, dist, ids, wm, wo, radial, cot, frag,
    node_o, gmsg_o, gout_o, outer_o,
    wmb, wob, idb, fx, cotb, srcb, distb, part_r,
    rim_lo, rim_hi, xo, xm, yo, ym, oo, om,
    bas, mtv, mtc, mc, ps, act, dsl, act_t, feats_t, dout, rr, spread, dproj,
    part_s, rim_s, so, ko, sm, km, syo, sym, gf, tb,
    loc, s_wy, r_wy, s_iy, r_iy, s_oy, r_oy, s_wx, r_wx, s_ix, r_ix, s_ox, r_ox,
    s_misc, r_misc, s_xo, r_xo, s_xm, r_xm, s_yo, r_yo, s_ym, r_ym, s_oo, r_oo, s_om, r_om,
):
    r = lax.axis_index("replica")
    f = lax.axis_index("fsdp")
    ylo, z = r // 8, r % 8
    h, x, c = f // 8, (f // 2) % 4, f % 2
    q = f // 2
    s = 2 * ylo - 1
    xp, xn, x2 = (x + 1) % 4, (x + 3) % 4, (x + 2) % 4
    ha, hb, h2 = (h + s + 4) % 4, (h - s + 4) % 4, (h + 2) % 4
    half = h // 2

    def dev(ylo_, h_, x_, c_):
        return (ylo_ * 8 + z, h_ * 8 + x_ * 2 + c_)

    def chip(q_, c_):
        return (r, q_ * 2 + c_)

    partner = dev(ylo, h, x, 1 - c)
    right, left = dev(ylo, h, xp, c), dev(ylo, h, xn, c)
    qn, qp = (q + 1) % 16, (q + 15) % 16
    y_to = ((1 - ylo, ha), (ylo, ha), (1 - ylo, h2))
    y_in = (ha, hb, h2)
    y_from = ((1 - ylo, ha), (ylo, hb), (1 - ylo, h2))

    def send(a_, b_, ss, rs, to):
        cp = pltpu.make_async_remote_copy(
            src_ref=a_, dst_ref=b_, send_sem=ss, recv_sem=rs, device_id=to, device_id_type=MESH
        )
        cp.start()
        return cp

    def arrived(b_, ss, rs, frm):
        pltpu.make_async_remote_copy(
            src_ref=b_, dst_ref=b_, send_sem=ss, recv_sem=rs, device_id=frm, device_id_type=MESH
        ).wait_recv()

    bar = pltpu.get_barrier_semaphore()
    greet = [partner, right, left]
    for c_ in (0, 1):
        greet += [
            dev(ylo, ha, x, c_), dev(ylo, hb, x, c_), dev(ylo, h2, x, c_),
            dev(1 - ylo, ha, x, c_), dev(1 - ylo, h2, x, c_), chip(qn, c_), chip(qp, c_),
        ]
    greet += [((r + d) % 16, f) for d in range(1, 16)]
    for g in greet:
        pl.semaphore_signal(bar, inc=1, device_id=g, device_id_type=MESH)

    own = [
        pltpu.make_async_copy(
            wm.at[:, pl.ds(pl.multiple_of(c * HC, HC), HC)], wmb.at[h, x, c], loc.at[0]
        ),
        pltpu.make_async_copy(ids, idb.at[h, x, c], loc.at[1]),
        pltpu.make_async_copy(
            feats, fx.at[pl.ds(pl.multiple_of(H + A * c, H), A)], loc.at[2]
        ),
        pltpu.make_async_copy(cot, cotb.at[c], loc.at[3]),
        pltpu.make_async_copy(src, srcb.at[c], loc.at[4]),
        pltpu.make_async_copy(dist, distb.at[c], loc.at[5]),
    ]
    for o in own:
        o.start()

    @pl.when(half == c)
    def _():
        cp = pltpu.make_async_copy(wo, wob.at[h % 2, x, c], loc.at[6])
        cp.start()
        cp.wait()

    @pl.when(q == 0)
    def _():
        fx[0:H, :] = jnp.zeros((H, C), BF16)
        rim_lo[...] = jnp.zeros((H, HC), BF16)

    @pl.when(q == 15)
    def _():
        fx[H + 2 * A :, :] = jnp.zeros((H, C), BF16)
        rim_hi[...] = jnp.zeros((H, HC), BF16)

    for o in own:
        o.wait()
    pl.semaphore_wait(bar, len(greet))

    sent = []
    other = pl.ds(pl.multiple_of((1 - c) * HC, HC), HC)
    mine_c = pl.ds(pl.multiple_of(c * HC, HC), HC)
    sent.append(send(wm.at[:, other], wmb.at[h, x, c], s_wy.at[6], r_wy.at[6], partner))
    sent.append(send(ids, idb.at[h, x, c], s_iy.at[6], r_iy.at[6], partner))
    for j, (yl, hh) in enumerate(y_to):
        for c_ in (0, 1):
            to = dev(yl, hh, x, c_)
            sent.append(
                send(
                    wm.at[:, pl.ds(c_ * HC, HC)], wmb.at[h, x, c],
                    s_wy.at[2 * j + c_], r_wy.at[2 * j + c], to,
                )
            )
    for j, hh in enumerate((hb, ha, h2)):
        for c_ in (0, 1):
            sent.append(
                send(
                    ids, idb.at[h, x, c], s_iy.at[2 * j + c_], r_iy.at[2 * j + c],
                    dev(ylo, hh, x, c_),
                )
            )
    sent.append(send(src, srcb.at[c], s_misc.at[0], r_misc.at[0], partner))
    sent.append(send(dist, distb.at[c], s_misc.at[1], r_misc.at[1], partner))
    f_rows = pl.ds(pl.multiple_of(H + A * c, H), A)
    sent.append(send(feats, fx.at[f_rows], s_misc.at[2], r_misc.at[2], partner))
    sent.append(send(cot, cotb.at[c], s_misc.at[3], r_misc.at[3], partner))

    up_ok = jnp.logical_and(c == 1, q < 15)
    dn_ok = jnp.logical_and(c == 0, q > 0)

    def up_copy(c_):
        return pltpu.make_async_remote_copy(
            src_ref=feats.at[pl.ds(A - H, H)], dst_ref=fx.at[pl.ds(0, H)],
            send_sem=s_misc.at[4 + c_], recv_sem=r_misc.at[4],
            device_id=chip(qn, c_), device_id_type=MESH,
        )

    def dn_copy(c_):
        return pltpu.make_async_remote_copy(
            src_ref=feats.at[pl.ds(0, H)], dst_ref=fx.at[pl.ds(H + 2 * A, H)],
            send_sem=s_misc.at[4 + c_], recv_sem=r_misc.at[5],
            device_id=chip(qp, c_), device_id_type=MESH,
        )

    @pl.when(up_ok)
    def _():
        for c_ in (0, 1):
            up_copy(c_).start()

    @pl.when(dn_ok)
    def _():
        for c_ in (0, 1):
            dn_copy(c_).start()

    for j, (yl, hh) in enumerate(y_to):
        sent.append(
            send(
                wo, wob.at[h % 2, x, c], s_oy.at[j], r_oy.at[2 * j + c], dev(yl, hh, x, half)
            )
        )

    def wo_partner():
        return pltpu.make_async_remote_copy(
            src_ref=wo, dst_ref=wob.at[h % 2, x, c], send_sem=s_oy.at[3], recv_sem=r_oy.at[6],
            device_id=partner, device_id_type=MESH,
        )

    @pl.when(half != c)
    def _():
        wo_partner().start()

    def wm_forward(k):
        yb = h if k == 0 else y_in[k - 1]
        if k == 0:
            arrived(wmb.at[h, x, 1 - c], s_wy.at[6], r_wy.at[6], partner)
            arrived(idb.at[h, x, 1 - c], s_iy.at[6], r_iy.at[6], partner)
        else:
            for c_ in (0, 1):
                frm = dev(*y_from[k - 1], x, c_)
                i = 2 * (k - 1) + c_
                arrived(wmb.at[yb, x, c_], s_wy.at[i], r_wy.at[i], frm)
                arrived(idb.at[yb, x, c_], s_iy.at[i], r_iy.at[i], dev(ylo, yb, x, c_))
        for i, to in enumerate((right, left)):
            sent.append(send(wmb.at[yb, x], wmb.at[yb, x], s_wx.at[k, i], r_wx.at[k, i], to))
            sent.append(send(idb.at[yb, x], idb.at[yb, x], s_ix.at[k, i], r_ix.at[k, i], to))

    def wm_relay(k):
        yb = h if k == 0 else y_in[k - 1]
        arrived(wmb.at[yb, xn], s_wx.at[k, 0], r_wx.at[k, 0], left)
        arrived(idb.at[yb, xn], s_ix.at[k, 0], r_ix.at[k, 0], left)
        if k % 2:
            arrived(wmb.at[yb, xp], s_wx.at[k, 1], r_wx.at[k, 1], right)
            arrived(idb.at[yb, xp], s_ix.at[k, 1], r_ix.at[k, 1], right)
        xs, to = (xp, left) if k % 2 else (xn, right)
        sent.append(send(wmb.at[yb, xs], wmb.at[yb, xs], s_wx.at[k, 2], r_wx.at[k, 2], to))
        sent.append(send(idb.at[yb, xs], idb.at[yb, xs], s_ix.at[k, 2], r_ix.at[k, 2], to))

    def wm_finish(k):
        yb = h if k == 0 else y_in[k - 1]
        frm = right if k % 2 else left
        if not k % 2:
            arrived(wmb.at[yb, xp], s_wx.at[k, 1], r_wx.at[k, 1], right)
            arrived(idb.at[yb, xp], s_ix.at[k, 1], r_ix.at[k, 1], right)
        arrived(wmb.at[yb, x2], s_wx.at[k, 2], r_wx.at[k, 2], frm)
        arrived(idb.at[yb, x2], s_ix.at[k, 2], r_ix.at[k, 2], frm)

    norm = 1.0 / math.sqrt(NB)

    def build(p):
        d = distb[p]
        env = 0.5 * (jnp.cos(d * (math.pi / 5.0)) + 1.0) * norm
        for b in range(BASIS):
            bas[b] = jnp.exp(-2.0 * (d - 5.0 * b / (BASIS - 1)) ** 2) * env
        base = 2 * A * q - H + A * p

        def tile(t, carry):
            row = pl.multiple_of(t * 16, 16)
            at = row + base + lax.broadcasted_iota(jnp.int32, (16, A), 0)
            accs = [jnp.zeros((16, A), F32) for _ in range(BASIS)]
            for k in range(NB):
                hit = srcb[p, k : k + 1, :] == at
                for b in range(BASIS):
                    accs[b] = accs[b] + jnp.where(hit, bas[b, k : k + 1, :], 0.0)
            for b in range(BASIS):
                mtv[pl.ds(pl.multiple_of(b * W + row, 16), 16), :] = accs[b]
                mtc[p, pl.ds(row, 16), b * A : (b + 1) * A] = accs[b].astype(BF16)
            return carry

        lax.fori_loop(0, W // 16, tile, 0)
        for t in range(BASIS * W // A):
            mc[p, :, t * A : (t + 1) * A] = mtv[t * A : (t + 1) * A, :].T.astype(BF16)

    wm_forward(0)
    arrived(srcb.at[1 - c], s_misc.at[0], r_misc.at[0], partner)
    arrived(distb.at[1 - c], s_misc.at[1], r_misc.at[1], partner)
    build(0)
    wm_forward(1)
    wm_forward(2)
    wm_relay(0)
    build(1)
    wm_forward(3)
    wm_relay(1)
    wm_relay(2)

    for k in range(3):
        @pl.when(y_in[k] // 2 == c)
        def _(k=k):
            for c_ in (0, 1):
                i = 2 * k + c_
                arrived(
                    wob.at[y_in[k] % 2, x, c_], s_oy.at[0], r_oy.at[i], dev(*y_from[k], x, c_)
                )

    @pl.when(half == c)
    def _():
        arrived(wob.at[h % 2, x, 1 - c], s_oy.at[3], r_oy.at[6], partner)

    for e in (0, 1):
        for i, to in enumerate((right, left)):
            sent.append(send(wob.at[e, x], wob.at[e, x], s_ox.at[e, i], r_ox.at[e, i], to))
    wm_relay(3)

    arrived(fx.at[pl.ds(pl.multiple_of(H + A * (1 - c), H), A)], s_misc.at[2], r_misc.at[2], partner)
    for p in (0, 1):
        feats_t[:, :, :, p * A : (p + 1) * A] = (
            fx[H + p * A : H + (p + 1) * A, :].T.reshape(4, 4, 64, A)
        )
    arrived(cotb.at[1 - c], s_misc.at[3], r_misc.at[3], partner)

    @pl.when(q > 0)
    def _():
        arrived(fx.at[pl.ds(0, H)], s_misc.at[4], r_misc.at[4], chip(qp, 1))

    @pl.when(q < 15)
    def _():
        arrived(fx.at[pl.ds(H + 2 * A, H)], s_misc.at[4], r_misc.at[5], chip(qn, 0))

    for k in range(4):
        wm_finish(k)

    all_ids = idb[...].reshape(32, A)
    for p in (0, 1):
        mine = idb[h, x, p]
        wrow = jnp.zeros((1, A), F32)
        for g in range(GRAPHS):
            count = jnp.sum((all_ids == g).astype(F32), axis=0, keepdims=True)
            count = jnp.sum(count, axis=1, keepdims=True)
            wrow = wrow + jnp.where(mine == g, lax.rsqrt(jnp.broadcast_to(count, (1, A))), 0.0)
        wcol = jnp.broadcast_to(wrow, (A, A)).T
        for t in range(C // A):
            cols = slice(t * A, (t + 1) * A)
            dout[p * A : (p + 1) * A, cols] = (cotb[p, :, cols].astype(F32) * wcol).astype(BF16)

    wmat = wmb[...].reshape(C, HC)
    proj = jnp.dot(fx[...], wmat, preferred_element_type=F32).astype(BF16)
    spread[...] = proj.astype(F32)
    for p in (0, 1):
        for b in range(BASIS):
            ps[b * W : (b + 1) * W, :] = (
                spread[p * A : p * A + W, :] * radial[b : b + 1, mine_c]
            ).astype(BF16)
        agg = jnp.dot(mc[p], ps[...], preferred_element_type=F32)
        sig = 1.0 / (1.0 + jnp.exp(-agg))
        a16 = (agg * sig).astype(BF16)
        rows = slice(p * A, (p + 1) * A)
        act[rows, :] = a16
        dsl[rows, :] = sig * (1.0 + agg * (1.0 - sig))
        act_t[:, :, :, rows] = a16.T.reshape(2, 4, 64, A)

    def out_part(xd):
        return jnp.dot(
            act_t[:, pl.ds(xd, 1)].reshape(A, 2 * A), dout[...], preferred_element_type=F32
        )

    v = out_part(x2)
    so[0] = v[:64].astype(BF16)
    so[1] = v[64:].astype(BF16)
    sent.append(send(so.at[0], xo.at[0], s_xo.at[0], r_xo.at[0], right))
    sent.append(send(so.at[1], xo.at[1], s_xo.at[1], r_xo.at[1], left))
    v = out_part(xp)
    ko[0] = v[:64]
    so[2] = v[64:].astype(BF16)
    sent.append(send(so.at[2], xo.at[2], s_xo.at[2], r_xo.at[2], right))
    v = out_part(xn)
    so[3] = v[:64].astype(BF16)
    ko[1] = v[64:]
    sent.append(send(so.at[3], xo.at[3], s_xo.at[3], r_xo.at[3], left))
    v = out_part(x)
    ko[2] = v[:64]
    ko[3] = v[64:]

    for e in (0, 1):
        if e == 0:
            arrived(wob.at[0, xn], s_ox.at[0, 0], r_ox.at[0, 0], left)
            sent.append(send(wob.at[0, xn], wob.at[0, xn], s_ox.at[0, 2], r_ox.at[0, 2], right))
        else:
            arrived(wob.at[1, xp], s_ox.at[1, 1], r_ox.at[1, 1], right)
            sent.append(send(wob.at[1, xp], wob.at[1, xp], s_ox.at[1, 2], r_ox.at[1, 2], left))
    arrived(wob.at[0, xp], s_ox.at[0, 1], r_ox.at[0, 1], right)
    arrived(wob.at[1, xn], s_ox.at[1, 0], r_ox.at[1, 0], left)
    arrived(wob.at[0, x2], s_ox.at[0, 2], r_ox.at[0, 2], left)
    arrived(wob.at[1, x2], s_ox.at[1, 2], r_ox.at[1, 2], right)

    womat = wob[...].reshape(HC, C)
    for p in (0, 1):
        rows = slice(p * A, (p + 1) * A)
        dagg = contract(dout[rows, :], womat, 1, 1) * dsl[rows, :]
        for b in range(BASIS):
            rr[b * A : (b + 1) * A, :] = (dagg * radial[b : b + 1, mine_c]).astype(BF16)
        part = jnp.dot(mtc[p], rr[...], preferred_element_type=F32)
        if p == 0:
            spread[0:W, :] = part
            rim_s[0] = part[:H].astype(BF16)
        else:
            spread[A:W, :] = spread[A:W, :] + part[: W - A]
            spread[W:, :] = part[W - A :]
            rim_s[1] = part[W - H :].astype(BF16)

    def rim_dn():
        return pltpu.make_async_remote_copy(
            src_ref=rim_s.at[0], dst_ref=rim_hi, send_sem=s_misc.at[6], recv_sem=r_misc.at[6],
            device_id=chip(qp, c), device_id_type=MESH,
        )

    def rim_up():
        return pltpu.make_async_remote_copy(
            src_ref=rim_s.at[1], dst_ref=rim_lo, send_sem=s_misc.at[7], recv_sem=r_misc.at[7],
            device_id=chip(qn, c), device_id_type=MESH,
        )

    @pl.when(q > 0)
    def _():
        rim_dn().start()

    @pl.when(q < 15)
    def _():
        rim_up().start()

    arrived(xo.at[0], s_xo.at[0], r_xo.at[0], left)
    so[4] = (ko[0] + xo[0].astype(F32)).astype(BF16)
    sent.append(send(so.at[4], xo.at[4], s_xo.at[4], r_xo.at[4], right))
    arrived(xo.at[1], s_xo.at[1], r_xo.at[1], right)
    so[5] = (ko[1] + xo[1].astype(F32)).astype(BF16)
    sent.append(send(so.at[5], xo.at[5], s_xo.at[5], r_xo.at[5], left))

    @pl.when(q > 0)
    def _():
        arrived(rim_lo, s_misc.at[7], r_misc.at[7], chip(qp, c))

    @pl.when(q < 15)
    def _():
        arrived(rim_hi, s_misc.at[6], r_misc.at[6], chip(qn, c))

    dproj[0:H, :] = (spread[H : 2 * H, :] + rim_lo[...].astype(F32)).astype(BF16)
    dproj[H : 2 * A - H, :] = spread[2 * H : 2 * A, :].astype(BF16)
    dproj[2 * A - H :, :] = (spread[2 * A : 2 * A + H, :] + rim_hi[...].astype(F32)).astype(BF16)

    def msg_part(xd):
        v_ = jnp.dot(
            feats_t[:, pl.ds(xd, 1)].reshape(2 * A, 2 * A), dproj[...], preferred_element_type=F32
        )
        return v_[:A], v_[A:]

    lo, hi = msg_part(x2)
    sm[0] = lo.astype(BF16)
    sm[1] = hi.astype(BF16)
    sent.append(send(sm.at[0], xm.at[0], s_xm.at[0], r_xm.at[0], right))
    sent.append(send(sm.at[1], xm.at[1], s_xm.at[1], r_xm.at[1], left))
    lo, hi = msg_part(xp)
    km[0] = lo
    sm[2] = hi.astype(BF16)
    sent.append(send(sm.at[2], xm.at[2], s_xm.at[2], r_xm.at[2], right))
    lo, hi = msg_part(xn)
    sm[3] = lo.astype(BF16)
    km[1] = hi
    sent.append(send(sm.at[3], xm.at[3], s_xm.at[3], r_xm.at[3], left))
    lo, hi = msg_part(x)
    km[2] = lo
    km[3] = hi

    arrived(xo.at[3], s_xo.at[3], r_xo.at[3], right)
    arrived(xo.at[4], s_xo.at[4], r_xo.at[4], left)
    arrived(xo.at[2], s_xo.at[2], r_xo.at[2], left)
    arrived(xo.at[5], s_xo.at[5], r_xo.at[5], right)
    syo[0] = (ko[2] + xo[3].astype(F32) + xo[4].astype(F32)).astype(BF16).reshape(2, 32, C)
    syo[1] = (ko[3] + xo[2].astype(F32) + xo[5].astype(F32)).astype(BF16).reshape(2, 32, C)

    def yo_copy(e, c_):
        return pltpu.make_async_remote_copy(
            src_ref=syo.at[e, c_], dst_ref=yo.at[h],
            send_sem=s_yo.at[2 * e + c_], recv_sem=r_yo.at[h],
            device_id=dev(ylo, 2 * c + e, x, c_), device_id_type=MESH,
        )

    for e in (0, 1):
        for c_ in (0, 1):
            is_me = jnp.logical_and(2 * c + e == h, c == c_)

            @pl.when(jnp.logical_not(is_me))
            def _(e=e, c_=c_):
                yo_copy(e, c_).start()

            @pl.when(is_me)
            def _(e=e, c_=c_):
                cp = pltpu.make_async_copy(syo.at[e, c_], yo.at[h], loc.at[7])
                cp.start()
                cp.wait()

    womat = wob[...].reshape(HC, C)
    a_other = act[pl.ds(pl.multiple_of((1 - c) * A, A), A), :]
    part_s[...] = jnp.dot(a_other, womat, preferred_element_type=F32).astype(BF16)
    sent.append(send(part_s, part_r, s_misc.at[8], r_misc.at[8], partner))
    a_own = act[pl.ds(pl.multiple_of(c * A, A), A), :]
    node_own = jnp.dot(a_own, womat, preferred_element_type=F32) + feats[...].astype(F32)

    arrived(xm.at[0], s_xm.at[0], r_xm.at[0], left)
    sm[4] = (km[0] + xm[0].astype(F32)).astype(BF16)
    sent.append(send(sm.at[4], xm.at[4], s_xm.at[4], r_xm.at[4], right))
    arrived(xm.at[1], s_xm.at[1], r_xm.at[1], right)
    sm[5] = (km[1] + xm[1].astype(F32)).astype(BF16)
    sent.append(send(sm.at[5], xm.at[5], s_xm.at[5], r_xm.at[5], left))

    arrived(part_r, s_misc.at[8], r_misc.at[8], partner)
    node_o[...] = (node_own + part_r[...].astype(F32)).astype(BF16)

    for h_ in range(4):
        @pl.when(jnp.logical_or(h_ != h, c != half))
        def _(h_=h_):
            arrived(yo.at[h_], s_yo.at[0], r_yo.at[h_], dev(ylo, h_, x, half))

    total = yo[0].astype(F32) + yo[1].astype(F32) + yo[2].astype(F32) + yo[3].astype(F32)
    gout_o[0] = total.astype(BF16)
    gf[...] = total
    chosen = jnp.full((32, FRAG), frag[0], jnp.int32)

    def decoded():
        piece = jnp.zeros((32, FRAG), F32)
        for b in range(C // FRAG):
            piece = jnp.where(chosen == b, gf[:, b * FRAG : (b + 1) * FRAG], piece)
        scale = (jnp.max(jnp.abs(piece), axis=1, keepdims=True) + TINY).astype(BF16).astype(F32)
        code = (piece / scale).astype(BF16).astype(F32)
        return (scale * code).astype(BF16)

    def outer_send(m, buf, ss, rs):
        for d in range(1, 16):
            sent.append(send(tb.at[m], buf.at[r], ss.at[d], rs.at[d], ((r + d) % 16, f)))

    def outer_sum(m, buf, ss, rs):
        for d in range(1, 16):
            r_ = (r + 16 - d) % 16
            arrived(buf.at[r_], ss.at[d], rs.at[d], (r_, f))
        outer_o[m] = jnp.sum(buf[...].astype(F32), axis=0)

    term = decoded()
    tb[1] = term
    oo[r] = term
    outer_send(1, oo, s_oo, r_oo)

    arrived(xm.at[3], s_xm.at[3], r_xm.at[3], right)
    arrived(xm.at[4], s_xm.at[4], r_xm.at[4], left)
    arrived(xm.at[2], s_xm.at[2], r_xm.at[2], left)
    arrived(xm.at[5], s_xm.at[5], r_xm.at[5], right)
    lo = (km[2] + xm[3].astype(F32) + xm[4].astype(F32)).astype(BF16)
    hi = (km[3] + xm[2].astype(F32) + xm[5].astype(F32)).astype(BF16)
    sym[0:2] = lo.reshape(2, 2, 32, HC)
    sym[2:4] = hi.reshape(2, 2, 32, HC)
    keep = pltpu.make_async_copy(sym.at[h, c], ym.at[h, c], loc.at[8])
    keep.start()
    for d in range(7, 0, -1):
        hh, c_ = (h + d // 2) % 4, (c + d) % 2
        sent.append(
            send(sym.at[hh, c_], ym.at[h, c], s_ym.at[d], r_ym.at[d], dev(ylo, hh, x, c_))
        )
    outer_sum(1, oo, s_oo, r_oo)
    keep.wait()
    for d in range(1, 8):
        hh, c_ = (h + 4 - d // 2) % 4, (c + d) % 2
        arrived(ym.at[hh, c_], s_ym.at[d], r_ym.at[d], dev(ylo, hh, x, c_))
    for c_ in (0, 1):
        total = (
            ym[0, c_].astype(F32) + ym[1, c_].astype(F32)
            + ym[2, c_].astype(F32) + ym[3, c_].astype(F32)
        )
        gf[:, c_ * HC : (c_ + 1) * HC] = total
        gmsg_o[0, :, c_ * HC : (c_ + 1) * HC] = total.astype(BF16)
    term = decoded()
    tb[0] = term
    om[r] = term
    outer_send(0, om, s_om, r_om)
    outer_sum(0, om, s_om, r_om)

    for cp in sent:
        cp.wait_send()

    @pl.when(up_ok)
    def _():
        for c_ in (0, 1):
            up_copy(c_).wait_send()

    @pl.when(dn_ok)
    def _():
        for c_ in (0, 1):
            dn_copy(c_).wait_send()

    @pl.when(half != c)
    def _():
        wo_partner().wait_send()

    @pl.when(q > 0)
    def _():
        rim_dn().wait_send()

    @pl.when(q < 15)
    def _():
        rim_up().wait_send()

    for e in (0, 1):
        for c_ in (0, 1):
            @pl.when(jnp.logical_not(jnp.logical_and(2 * c + e == h, c == c_)))
            def _(e=e, c_=c_):
                yo_copy(e, c_).wait_send()


def shards(feats, src, dist, ids, wm, wo, radial, cot, frag):
    vm = pl.BlockSpec(memory_space=pltpu.VMEM)
    dma = lambda *n: pltpu.SemaphoreType.DMA(n)
    V = pltpu.VMEM
    return pl.pallas_call(
        body,
        out_shape=(
            jax.ShapeDtypeStruct((A, C), BF16),
            jax.ShapeDtypeStruct((1, 32, C), BF16),
            jax.ShapeDtypeStruct((1, 32, C), BF16),
            jax.ShapeDtypeStruct((2, 32, FRAG), F32),
        ),
        in_specs=[vm] * 8 + [pl.BlockSpec(memory_space=pltpu.SMEM)],
        out_specs=(vm,) * 4,
        scratch_shapes=[
            V((4, 4, 2, 32, HC), BF16),
            V((2, 4, 2, 32, C), BF16),
            V((4, 4, 2, 1, A), jnp.int32),
            V((EXT, C), BF16),
            V((2, A, C), BF16),
            V((2, NB, A), jnp.int32),
            V((2, NB, A), F32),
            V((A, C), BF16),
            V((H, HC), BF16),
            V((H, HC), BF16),
            V((6, 64, C), BF16),
            V((6, A, HC), BF16),
            V((4, 32, C), BF16),
            V((4, 2, 32, HC), BF16),
            V((16, 32, FRAG), BF16),
            V((16, 32, FRAG), BF16),
            V((BASIS, NB, A), F32),
            V((BASIS * W, A), F32),
            V((2, W, BASIS * A), BF16),
            V((2, A, BASIS * W), BF16),
            V((BASIS * W, HC), BF16),
            V((2 * A, HC), BF16),
            V((2 * A, HC), F32),
            V((2, 4, 64, 2 * A), BF16),
            V((4, 4, 64, 2 * A), BF16),
            V((2 * A, C), BF16),
            V((BASIS * A, HC), BF16),
            V((EXT, HC), F32),
            V((2 * A, HC), BF16),
            V((A, C), BF16),
            V((2, H, HC), BF16),
            V((6, 64, C), BF16),
            V((4, 64, C), F32),
            V((6, A, HC), BF16),
            V((4, A, HC), F32),
            V((2, 2, 32, C), BF16),
            V((4, 2, 32, HC), BF16),
            V((32, C), F32),
            V((2, 32, FRAG), BF16),
            dma(9),
            dma(7), dma(7), dma(7), dma(7), dma(4), dma(7),
            dma(4, 3), dma(4, 3), dma(4, 3), dma(4, 3), dma(2, 3), dma(2, 3),
            dma(9), dma(9), dma(6), dma(6), dma(6), dma(6),
            dma(4), dma(4), dma(8), dma(8), dma(16), dma(16), dma(16), dma(16),
        ],
        compiler_params=pltpu.CompilerParams(
            collective_id=0, has_side_effects=True, vmem_limit_bytes=56 << 20
        ),
        name="step",
    )(feats, src, dist, ids, wm, wo, radial, cot, frag)


def solution(mesh):
    placed = (
        P(("replica", "fsdp"), None),
        P(None, ("replica", "fsdp")),
        P(None, ("replica", "fsdp")),
        P("replica", "fsdp"),
        P("fsdp", None),
        P("fsdp", None),
        P(),
        P(("replica", "fsdp"), None),
        P(),
    )
    return jax.shard_map(
        shards,
        mesh=mesh,
        in_specs=placed,
        out_specs=(
            P(("replica", "fsdp"), None),
            P("replica", "fsdp", None),
            P("replica", "fsdp", None),
            P(None, "fsdp", None),
        ),
        check_vma=False,
    )
```

time: 415 us -> 89.9 us (0.22)
  the two profiles are of different devices: /device:TPU:8 before, /device:TPU:3 now
where the time goes in v1:
time: 89.9 us; the launch traced here: 89.6 us
  Pallas kernels  84.4 us (94%)
  local copies, waits for them, and re-layouts  3.94 us (4%)
  between operations  1.3 us (1%)
    pallas_call x1, Pallas kernels, shards(): pl.pallas_call(body, out_shape=(jax.ShapeDtypeStruct((A, C), BF16), jax.S...  84.4 us
    unnamed x10, local copies, waits for them, and re-layouts  3.94 us

profile of v1, /device:TPU:3, one launch (start us, length us, event | category | flops | bytes accessed | tf_op | source)
XLA Modules:
  0.0 89.6 jit_solution(10592546806183020225)
XLA Ops:
  1.3 84.4 %step.1 = (bf16[128,1024]{1,0:T(8,128)(2,1)}, bf16[1,32,1024]{2,1,0:T(8,128)(2,1)}, bf16[1,32,1024]{2,1,0:T(8,128)(2,1)}, f32[2,32,128]{2,1,0:T(8,128)}) custom-call(bf16[128,1024]{1,0:T(8,128)(2,1)} %feats.1, s32[12,128]{1,0:T(8,128)} %src.1, f32[12,128]{1,0:T(8,128)} %dist.1, s32[1,128]{1,0:T(1,128)} %ids.1, bf16[32,1024]{1,0:T(8,128)(2,1)} %wm.1, ...), custom_call_target="tpu_custom_call" | custom-call | tf_op jit(solution)/shard_map/step/pallas_call | solution.py:590
  85.7 0.0 copy-start.1
  85.7 1.7 %copy.18 = bf16[128,1024]{1,0:T(8,128)(2,1)} copy(bf16[128,1024]{1,0:T(8,128)(2,1)} %get-tuple-element.8) | data formatting | bytes 524288
  87.4 0.0 copy-done.1
  87.4 0.0 copy-start
  87.4 0.6 copy.19
  88.0 0.2 copy-done
  88.3 0.0 copy-start.2
  88.3 0.6 copy.20
  88.9 0.1 copy-done.2
  89.0 0.6 copy.21
Async XLA Ops:
  85.7 1.7 %copy-start.1 = (bf16[1,32,1024]{2,1,0:T(8,128)(2,1)S(1)}, bf16[1,32,1024]{2,1,0:T(8,128)(2,1)}, u32[]{:S(2)}) copy-start(bf16[1,32,1024]{2,1,0:T(8,128)(2,1)} %get-tuple-element.9) | copy-start | bytes 196612
  87.4 0.9 copy-start
  88.3 0.8 copy-start.2

commit v2 on v1

v2 whole, which is shorter than its diff:
```python
import functools
import math

import jax
import jax.numpy as jnp
from jax import lax
from jax.experimental import pallas as pl
from jax.experimental.pallas import tpu as pltpu
from jax.sharding import PartitionSpec as P

MESH = pl.DeviceIdType.MESH
F32 = jnp.float32
BF16 = jnp.bfloat16
GRAPHS = 8
FRAG = 128
A = 128
C = 1024
HC = 512
H = 32
NB = 12
BASIS = 8
W = 2 * A - 64
EXT = 2 * A + 2 * H
TINY = 1e-6


def contract(a, b, da, db):
    return lax.dot_general(a, b, (((da,), (db,)), ((), ())), preferred_element_type=F32)


def body(
    feats, src, dist, ids, wm, wo, radial_h, cot, frag,
    node_o, gmsg_o, gout_o, outer_o,
    wmb, wob, wmv, wov, radial, idb, fx, cotb, srcb, distb, part_r,
    rim_lo, rim_hi, xo, xm, yo, ym, oo, om,
    bas, mtv, mtc, mc, ps, act, dsl, act_t, feats_t, dout, rr, spread, dproj,
    part_s, rim_s, so, ko, sm, km, syo, sym, gf, gm, tb,
    loc, s_wy, r_wy, s_iy, r_iy, s_oy, r_oy, s_wx, r_wx, s_wz, r_wz, s_ix, r_ix,
    s_ox, r_ox, s_oz, r_oz,
    s_misc, r_misc, s_xo, r_xo, s_xm, r_xm, s_yo, r_yo, s_ym, r_ym, s_oo, r_oo, s_om, r_om,
):
    r = lax.axis_index("replica")
    f = lax.axis_index("fsdp")
    ylo, z = r // 8, r % 8
    h, x, c = f // 8, (f // 2) % 4, f % 2
    q = f // 2
    s = 2 * ylo - 1
    xp, xn, x2 = (x + 1) % 4, (x + 3) % 4, (x + 2) % 4
    ha, hb, h2 = (h + s + 4) % 4, (h - s + 4) % 4, (h + 2) % 4
    half = h // 2
    par = z % 2

    def dev(ylo_, h_, x_, c_):
        return (ylo_ * 8 + z, h_ * 8 + x_ * 2 + c_)

    def chip(q_, c_):
        return (r, q_ * 2 + c_)

    partner = dev(ylo, h, x, 1 - c)
    right, left = dev(ylo, h, xp, c), dev(ylo, h, xn, c)
    qn, qp = (q + 1) % 16, (q + 15) % 16
    y_to = ((1 - ylo, ha), (ylo, ha), (1 - ylo, h2))
    y_in = (ha, hb, h2)
    y_from = ((1 - ylo, ha), (ylo, hb), (1 - ylo, h2))

    def send(a_, b_, ss, rs, to):
        cp = pltpu.make_async_remote_copy(
            src_ref=a_, dst_ref=b_, send_sem=ss, recv_sem=rs, device_id=to, device_id_type=MESH
        )
        cp.start()
        return cp

    def arrived(b_, ss, rs, frm):
        pltpu.make_async_remote_copy(
            src_ref=b_, dst_ref=b_, send_sem=ss, recv_sem=rs, device_id=frm, device_id_type=MESH
        ).wait_recv()

    bar = pltpu.get_barrier_semaphore()
    greet = [partner]
    for c_ in (0, 1):
        greet += [dev(ylo, h, x_, c_) for x_ in (xp, xn, x2)]
        greet += [
            dev(ylo, ha, x, c_), dev(ylo, hb, x, c_), dev(ylo, h2, x, c_),
            dev(1 - ylo, ha, x, c_), dev(1 - ylo, h2, x, c_), chip(qn, c_), chip(qp, c_),
        ]
    greet += [((r + d) % 16, f) for d in range(1, 16)]
    for g in greet:
        pl.semaphore_signal(bar, inc=1, device_id=g, device_id_type=MESH)

    f_rows = pl.ds(pl.multiple_of(H + A * c, H), A)
    f_other = pl.ds(pl.multiple_of(H + A * (1 - c), H), A)
    own = [
        pltpu.make_async_copy(a_, b_, loc.at[i])
        for i, (a_, b_) in enumerate(
            (
                (wm, wmv),
                (wm.at[:, pl.ds(pl.multiple_of(c * HC, HC), HC)], wmb.at[h, x, c]),
                (ids, idb.at[h, x, c]),
                (src, srcb.at[c]),
                (dist, distb.at[c]),
                (feats, fx.at[f_rows]),
                (wo, wov),
                (cot, cotb.at[c]),
                (radial_h, radial),
            )
        )
    ]
    for o in own:
        o.start()

    @pl.when(half == c)
    def _():
        cp = pltpu.make_async_copy(wo, wob.at[h % 2, x, c], loc.at[9])
        cp.start()
        cp.wait()

    @pl.when(q == 0)
    def _():
        fx[0:H, :] = jnp.zeros((H, C), BF16)
        rim_lo[...] = jnp.zeros((H, HC), BF16)

    @pl.when(q == 15)
    def _():
        fx[H + 2 * A :, :] = jnp.zeros((H, C), BF16)
        rim_hi[...] = jnp.zeros((H, HC), BF16)

    for o in own:
        o.wait()
    pl.semaphore_wait(bar, len(greet))

    sent = []
    other = pl.ds(pl.multiple_of((1 - c) * HC, HC), HC)
    mine_c = pl.ds(pl.multiple_of(c * HC, HC), HC)
    sent.append(send(wmv.at[:, other], wmb.at[h, x, c], s_wy.at[6], r_wy.at[6], partner))

    def wm_y(j, c_):
        yl, hh = y_to[j]
        return pltpu.make_async_remote_copy(
            src_ref=wmv.at[:, pl.ds(c_ * HC, HC)], dst_ref=wmb.at[h, x, c],
            send_sem=s_wy.at[2 * j + c_], recv_sem=r_wy.at[2 * j + c],
            device_id=dev(yl, hh, x, c_), device_id_type=MESH,
        )

    def wo_y(j):
        yl, hh = y_to[j]
        return pltpu.make_async_remote_copy(
            src_ref=wov, dst_ref=wob.at[h % 2, x, c],
            send_sem=s_oy.at[j], recv_sem=r_oy.at[2 * j + c],
            device_id=dev(yl, hh, x, half), device_id_type=MESH,
        )

    y_of = ((2,), (0, 1))
    for parity in (0, 1):
        @pl.when(par == parity)
        def _(parity=parity):
            for j in y_of[parity]:
                for c_ in (0, 1):
                    wm_y(j, c_).start()

    @pl.when(h % 2 == par)
    def _():
        for j in (2, 1, 0):
            wo_y(j).start()

    sent.append(send(srcb.at[c], srcb.at[c], s_misc.at[0], r_misc.at[0], partner))
    sent.append(send(distb.at[c], distb.at[c], s_misc.at[1], r_misc.at[1], partner))
    my_ids = idb.at[h, x, c]
    sent.append(send(my_ids, my_ids, s_iy.at[6], r_iy.at[6], partner))
    for j, hh in enumerate((hb, ha, h2)):
        for c_ in (0, 1):
            sent.append(
                send(
                    my_ids, my_ids, s_iy.at[2 * j + c_], r_iy.at[2 * j + c], dev(ylo, hh, x, c_)
                )
            )

    def wm_in(k):
        if k == 0:
            arrived(wmb.at[h, x, 1 - c], s_wy.at[6], r_wy.at[6], partner)
        else:
            for c_ in (0, 1):
                i = 2 * (k - 1) + c_
                arrived(
                    wmb.at[y_in[k - 1], x, c_], s_wy.at[i], r_wy.at[i], dev(*y_from[k - 1], x, c_)
                )

    taken = ((h + par * s + 4) % 4, (h + 2 * (1 - par) - par * s + 4) % 4)
    rest = ((h + (1 - par) * s + 4) % 4, (h + 2 * par - (1 - par) * s + 4) % 4)
    z_to = ((ylo * 8 + (z + 1) % 8, f), (ylo * 8 + (z + 7) % 8, f))
    z_in = (z_to[1], z_to[0])

    far = dev(ylo, h, x2, c)

    def wm_x(n, i):
        ref = wmb.at[taken[n], x]
        return pltpu.make_async_remote_copy(
            src_ref=ref, dst_ref=ref, send_sem=s_wx.at[n, i], recv_sem=r_wx.at[n, i],
            device_id=(right, left, far)[i], device_id_type=MESH,
        )

    def wm_z(n, i, u):
        ref = wmb.at[taken[n], (xn, xp, x2, x)[i], u]
        return pltpu.make_async_remote_copy(
            src_ref=ref, dst_ref=ref, send_sem=s_wz.at[n, i, u], recv_sem=r_wz.at[n, i, u],
            device_id=z_to[u], device_id_type=MESH,
        )

    def wm_x_start(n, parity):
        @pl.when(par == parity)
        def _():
            if n or parity:
                wm_in(3 if parity == 0 else 1 + n)
            for i in range(3):
                wm_x(n, i).start()
            if n or parity:
                for u in (0, 1):
                    wm_z(n, 3, u).start()

    def wm_x_in(n, i):
        ref = wmb.at[taken[n], (xn, xp, x2)[i]]
        arrived(ref, s_wx.at[n, i], r_wx.at[n, i], (left, right, far)[i])
        for u in (0, 1):
            wm_z(n, i, u).start()

    norm = 1.0 / math.sqrt(NB)
    PARTS = 2

    def build(p, part):
        if part == 0:
            d = distb[p]
            env = 0.5 * (jnp.cos(d * (math.pi / 5.0)) + 1.0) * norm
            for b in range(BASIS):
                bas[b] = jnp.exp(-2.0 * (d - 5.0 * b / (BASIS - 1)) ** 2) * env
        base = 2 * A * q - H + A * p

        def tile(t, carry):
            row = pl.multiple_of(t * 16, 16)
            at = row + base + lax.broadcasted_iota(jnp.int32, (16, A), 0)
            accs = [jnp.zeros((16, A), F32) for _ in range(BASIS)]
            for k in range(NB):
                hit = srcb[p, k : k + 1, :] == at
                for b in range(BASIS):
                    accs[b] = accs[b] + jnp.where(hit, bas[b, k : k + 1, :], 0.0)
            for b in range(BASIS):
                mtv[pl.ds(pl.multiple_of(b * W + row, 16), 16), :] = accs[b]
                mtc[p, pl.ds(row, 16), b * A : (b + 1) * A] = accs[b].astype(BF16)
            return carry

        step = W // 16 // PARTS
        lax.fori_loop(part * step, (part + 1) * step, tile, 0)
        if part == PARTS - 1:
            for t in range(BASIS * W // A):
                mc[p, :, t * A : (t + 1) * A] = mtv[t * A : (t + 1) * A, :].T.astype(BF16)

    wm_in(0)
    wm_x_start(0, 0)

    def wo_partner():
        return pltpu.make_async_remote_copy(
            src_ref=wov, dst_ref=wob.at[h % 2, x, c], send_sem=s_oy.at[3], recv_sem=r_oy.at[6],
            device_id=partner, device_id_type=MESH,
        )

    @pl.when(half != c)
    def _():
        wo_partner().start()

    up_ok = jnp.logical_and(c == 1, q < 15)
    dn_ok = jnp.logical_and(c == 0, q > 0)

    def up_copy(c_):
        return pltpu.make_async_remote_copy(
            src_ref=fx.at[pl.ds(2 * A, H)], dst_ref=fx.at[pl.ds(0, H)],
            send_sem=s_misc.at[4 + c_], recv_sem=r_misc.at[4],
            device_id=chip(qn, c_), device_id_type=MESH,
        )

    def dn_copy(c_):
        return pltpu.make_async_remote_copy(
            src_ref=fx.at[pl.ds(H, H)], dst_ref=fx.at[pl.ds(H + 2 * A, H)],
            send_sem=s_misc.at[4 + c_], recv_sem=r_misc.at[5],
            device_id=chip(qp, c_), device_id_type=MESH,
        )

    @pl.when(up_ok)
    def _():
        for c_ in (0, 1):
            up_copy(c_).start()

    @pl.when(dn_ok)
    def _():
        for c_ in (0, 1):
            dn_copy(c_).start()

    sent.append(send(fx.at[f_rows], fx.at[f_rows], s_misc.at[2], r_misc.at[2], partner))
    sent.append(send(cotb.at[c], cotb.at[c], s_misc.at[3], r_misc.at[3], partner))

    def wo_in():
        @pl.when(h == 2 * c + par)
        def _():
            arrived(wob.at[par, x, 1 - c], s_oy.at[3], r_oy.at[6], partner)

        for j in range(3):
            @pl.when(y_in[j] == 2 * c + par)
            def _(j=j):
                for c_ in (0, 1):
                    arrived(
                        wob.at[par, x, c_], s_oy.at[0], r_oy.at[2 * j + c_],
                        dev(*y_from[j], x, c_),
                    )

        for i, to in enumerate((right, left, far)):
            ref = wob.at[par, x]
            sent.append(send(ref, ref, s_ox.at[i], r_ox.at[i], to))

    def wo_own_z(u):
        ref = wob.at[par, x, u]
        return pltpu.make_async_remote_copy(
            src_ref=ref, dst_ref=ref, send_sem=s_oz.at[3, u], recv_sem=r_oz.at[3, u],
            device_id=z_to[u], device_id_type=MESH,
        )

    def wo_z():
        @pl.when(h != 2 * c + par)
        def _():
            for u in (0, 1):
                wo_own_z(u).start()

    def wo_x_in(i):
        col = (xn, xp, x2)[i]
        arrived(wob.at[par, col], s_ox.at[i], r_ox.at[i], (left, right, far)[i])
        for u in (0, 1):
            ref = wob.at[par, col, u]
            sent.append(send(ref, ref, s_oz.at[i, u], r_oz.at[i, u], z_to[u]))

    arrived(srcb.at[1 - c], s_misc.at[0], r_misc.at[0], partner)
    arrived(distb.at[1 - c], s_misc.at[1], r_misc.at[1], partner)
    build(0, 0)
    wm_x_start(0, 1)
    wm_x_start(1, 0)
    wm_x_start(1, 1)
    arrived(idb.at[h, x, 1 - c], s_iy.at[6], r_iy.at[6], partner)
    for k, yb in enumerate(y_in):
        for c_ in (0, 1):
            i = 2 * k + c_
            arrived(idb.at[yb, x, c_], s_iy.at[i], r_iy.at[i], dev(ylo, yb, x, c_))
    for i, x_ in enumerate((xp, xn, x2)):
        ref = idb.at[:, x]
        sent.append(send(ref, ref, s_ix.at[i], r_ix.at[i], dev(ylo, h, x_, c)))
    build(0, 1)
    wo_in()
    wm_x_in(0, 0)
    wm_x_in(0, 1)
    build(1, 0)
    wm_x_in(0, 2)
    wm_x_in(1, 1)
    wm_x_in(1, 0)
    wm_x_in(1, 2)
    build(1, 1)
    arrived(fx.at[f_other], s_misc.at[2], r_misc.at[2], partner)
    for p in (0, 1):
        feats_t[:, :, :, p * A : (p + 1) * A] = (
            fx[H + p * A : H + (p + 1) * A, :].T.reshape(4, 4, 64, A)
        )
    arrived(cotb.at[1 - c], s_misc.at[3], r_misc.at[3], partner)

    @pl.when(q > 0)
    def _():
        arrived(fx.at[pl.ds(0, H)], s_misc.at[4], r_misc.at[4], chip(qp, 1))

    @pl.when(q < 15)
    def _():
        arrived(fx.at[pl.ds(H + 2 * A, H)], s_misc.at[4], r_misc.at[5], chip(qn, 0))

    wo_z()
    wo_x_in(0)
    wo_x_in(1)
    for i, x_ in enumerate((xn, xp, x2)):
        arrived(idb.at[:, x_], s_ix.at[i], r_ix.at[i], dev(ylo, h, x_, c))
    all_ids = idb[...].reshape(32, A)
    for p in (0, 1):
        mine = idb[h, x, p]
        wrow = jnp.zeros((1, A), F32)
        for g in range(GRAPHS):
            count = jnp.sum((all_ids == g).astype(F32), axis=0, keepdims=True)
            count = jnp.sum(count, axis=1, keepdims=True)
            wrow = wrow + jnp.where(mine == g, lax.rsqrt(jnp.broadcast_to(count, (1, A))), 0.0)
        wcol = jnp.broadcast_to(wrow, (A, A)).T
        for t in range(C // A):
            cols = slice(t * A, (t + 1) * A)
            dout[p * A : (p + 1) * A, cols] = (cotb[p, :, cols].astype(F32) * wcol).astype(BF16)

    for n in (0, 1):
        for i, col in enumerate((xn, xp, x2)):
            for u in (0, 1):
                arrived(wmb.at[rest[n], col, u], s_wz.at[n, i, u], r_wz.at[n, i, u], z_in[u])
        if n:
            for u in (0, 1):
                arrived(wmb.at[rest[n], x, u], s_wz.at[n, 3, u], r_wz.at[n, 3, u], z_in[u])
        else:
            @pl.when(par == 0)
            def _():
                for u in (0, 1):
                    arrived(wmb.at[rest[0], x, u], s_wz.at[0, 3, u], r_wz.at[0, 3, u], z_in[u])

    wmat = wmb[...].reshape(C, HC)
    proj = jnp.dot(fx[...], wmat, preferred_element_type=F32).astype(BF16)
    spread[...] = proj.astype(F32)
    for p in (0, 1):
        for b in range(BASIS):
            ps[b * W : (b + 1) * W, :] = (
                spread[p * A : p * A + W, :] * radial[b : b + 1, mine_c]
            ).astype(BF16)
        agg = jnp.dot(mc[p], ps[...], preferred_element_type=F32)
        sig = 1.0 / (1.0 + jnp.exp(-agg))
        a16 = (agg * sig).astype(BF16)
        rows = slice(p * A, (p + 1) * A)
        act[rows, :] = a16
        dsl[rows, :] = sig * (1.0 + agg * (1.0 - sig))
        act_t[:, :, :, rows] = a16.T.reshape(2, 4, 64, A)

    wo_x_in(2)
    def out_part(xd):
        return jnp.dot(
            act_t[:, pl.ds(xd, 1)].reshape(A, 2 * A), dout[...], preferred_element_type=F32
        )

    v = out_part(x2)
    so[0] = v[:64].astype(BF16)
    so[1] = v[64:].astype(BF16)
    sent.append(send(so.at[0], xo.at[0], s_xo.at[0], r_xo.at[0], right))
    sent.append(send(so.at[1], xo.at[1], s_xo.at[1], r_xo.at[1], left))
    v = out_part(xp)
    ko[0] = v[:64]
    so[2] = v[64:].astype(BF16)
    sent.append(send(so.at[2], xo.at[2], s_xo.at[2], r_xo.at[2], right))
    v = out_part(xn)
    so[3] = v[:64].astype(BF16)
    ko[1] = v[64:]
    sent.append(send(so.at[3], xo.at[3], s_xo.at[3], r_xo.at[3], left))
    v = out_part(x)
    ko[2] = v[:64]
    ko[3] = v[64:]

    arrived(xo.at[0], s_xo.at[0], r_xo.at[0], left)
    so[4] = (ko[0] + xo[0].astype(F32)).astype(BF16)
    sent.append(send(so.at[4], xo.at[4], s_xo.at[4], r_xo.at[4], right))
    arrived(xo.at[1], s_xo.at[1], r_xo.at[1], right)
    so[5] = (ko[1] + xo[1].astype(F32)).astype(BF16)
    sent.append(send(so.at[5], xo.at[5], s_xo.at[5], r_xo.at[5], left))

    for i, x_ in enumerate((xn, xp, x2)):
        for u in (0, 1):
            arrived(wob.at[1 - par, x_, u], s_oz.at[i, u], r_oz.at[i, u], z_in[u])

    @pl.when(h != 2 * c + 1 - par)
    def _():
        for u in (0, 1):
            arrived(wob.at[1 - par, x, u], s_oz.at[3, u], r_oz.at[3, u], z_in[u])

    @pl.when(h == 2 * c + 1 - par)
    def _():
        arrived(wob.at[1 - par, x, 1 - c], s_oy.at[3], r_oy.at[6], partner)

    womat = wob[...].reshape(HC, C)
    for p in (0, 1):
        rows = slice(p * A, (p + 1) * A)
        dagg = contract(dout[rows, :], womat, 1, 1) * dsl[rows, :]
        for b in range(BASIS):
            rr[b * A : (b + 1) * A, :] = (dagg * radial[b : b + 1, mine_c]).astype(BF16)
        part = jnp.dot(mtc[p], rr[...], preferred_element_type=F32)
        if p == 0:
            spread[0:W, :] = part
            rim_s[0] = part[:H].astype(BF16)
        else:
            spread[A:W, :] = spread[A:W, :] + part[: W - A]
            spread[W:, :] = part[W - A :]
            rim_s[1] = part[W - H :].astype(BF16)

    def rim_dn():
        return pltpu.make_async_remote_copy(
            src_ref=rim_s.at[0], dst_ref=rim_hi, send_sem=s_misc.at[6], recv_sem=r_misc.at[6],
            device_id=chip(qp, c), device_id_type=MESH,
        )

    def rim_up():
        return pltpu.make_async_remote_copy(
            src_ref=rim_s.at[1], dst_ref=rim_lo, send_sem=s_misc.at[7], recv_sem=r_misc.at[7],
            device_id=chip(qn, c), device_id_type=MESH,
        )

    @pl.when(q > 0)
    def _():
        rim_dn().start()

    @pl.when(q < 15)
    def _():
        rim_up().start()

    @pl.when(q > 0)
    def _():
        arrived(rim_lo, s_misc.at[7], r_misc.at[7], chip(qp, c))

    @pl.when(q < 15)
    def _():
        arrived(rim_hi, s_misc.at[6], r_misc.at[6], chip(qn, c))

    spread[H : 2 * H, :] = spread[H : 2 * H, :] + rim_lo[...].astype(F32)
    spread[2 * A : 2 * A + H, :] = spread[2 * A : 2 * A + H, :] + rim_hi[...].astype(F32)

    def turned(rows, back, blocks):
        which = jnp.full((rows, FRAG), frag[0], jnp.int32)
        res = []
        for k in range(4):
            v_ = blocks(k)
            for o in range(1, 4):
                hit = jnp.logical_or(which == o, which == o + 4)
                v_ = jnp.where(hit, blocks((k - o if back else k + o) % 4), v_)
            res.append(v_)
        return res

    for k, v in enumerate(
        turned(2 * A, False, lambda k: spread[H : H + 2 * A, k * FRAG : (k + 1) * FRAG])
    ):
        dproj[:, k * FRAG : (k + 1) * FRAG] = v.astype(BF16)

    def msg_part(xd, store_lo, store_hi):
        v_ = jnp.dot(
            feats_t[:, pl.ds(xd, 1)].reshape(2 * A, 2 * A), dproj[...], preferred_element_type=F32
        )
        for k in range(4):
            store_lo(k, v_[:A, k * FRAG : (k + 1) * FRAG])
            store_hi(k, v_[A:, k * FRAG : (k + 1) * FRAG])

    def staged(i):
        def f_(k, v_):
            sm[k, i] = v_.astype(BF16)
        return f_

    def kept(i):
        def f_(k, v_):
            km[k, i] = v_
        return f_

    msg_part(x2, staged(0), staged(1))
    msg_part(xp, kept(0), staged(2))
    msg_part(xn, staged(3), kept(1))
    msg_part(x, kept(2), kept(3))

    def msg_leg(k, i):
        to = (right, left, right, left, right, left)[i]
        sent.append(send(sm.at[k, i], xm.at[k, i], s_xm.at[k, i], r_xm.at[k, i], to))

    def msg_in(k, i):
        frm = (left, right, left, right, left, right)[i]
        arrived(xm.at[k, i], s_xm.at[k, i], r_xm.at[k, i], frm)

    def msg_first(k):
        for i in range(4):
            msg_leg(k, i)

    def msg_relay(k):
        for i in (0, 1):
            msg_in(k, i)
            sm[k, 4 + i] = (km[k, i] + xm[k, i].astype(F32)).astype(BF16)
            msg_leg(k, 4 + i)

    def msg_y(k):
        for i in (2, 3, 4, 5):
            msg_in(k, i)
        lo = (km[k, 2] + xm[k, 3].astype(F32) + xm[k, 4].astype(F32)).astype(BF16)
        hi = (km[k, 3] + xm[k, 2].astype(F32) + xm[k, 5].astype(F32)).astype(BF16)
        sym[k, 0:2] = lo.reshape(2, 2, 32, FRAG)
        sym[k, 2:4] = hi.reshape(2, 2, 32, FRAG)
        for d in range(7, 0, -1):
            hh, c_ = (h + d // 2) % 4, (c + d) % 2
            sent.append(
                send(
                    sym.at[k, hh, c_], ym.at[k, h, c], s_ym.at[k, d], r_ym.at[k, d],
                    dev(ylo, hh, x, c_),
                )
            )
        ym[k, h, c] = sym[k, h, c]

    def msg_sum(k):
        for d in range(1, 8):
            hh, c_ = (h + 4 - d // 2) % 4, (c + d) % 2
            arrived(ym.at[k, hh, c_], s_ym.at[k, d], r_ym.at[k, d], dev(ylo, hh, x, c_))
        for c_ in (0, 1):
            gm[c_, k] = (
                ym[k, 0, c_].astype(F32) + ym[k, 1, c_].astype(F32)
                + ym[k, 2, c_].astype(F32) + ym[k, 3, c_].astype(F32)
            )

    msg_first(0)
    msg_first(1)

    arrived(xo.at[3], s_xo.at[3], r_xo.at[3], right)
    arrived(xo.at[4], s_xo.at[4], r_xo.at[4], left)
    arrived(xo.at[2], s_xo.at[2], r_xo.at[2], left)
    arrived(xo.at[5], s_xo.at[5], r_xo.at[5], right)
    syo[0] = (ko[2] + xo[3].astype(F32) + xo[4].astype(F32)).astype(BF16).reshape(2, 32, C)
    syo[1] = (ko[3] + xo[2].astype(F32) + xo[5].astype(F32)).astype(BF16).reshape(2, 32, C)

    def yo_copy(e, c_):
        return pltpu.make_async_remote_copy(
            src_ref=syo.at[e, c_], dst_ref=yo.at[h],
            send_sem=s_yo.at[2 * e + c_], recv_sem=r_yo.at[h],
            device_id=dev(ylo, 2 * c + e, x, c_), device_id_type=MESH,
        )

    for e in (0, 1):
        for c_ in (0, 1):
            is_me = jnp.logical_and(2 * c + e == h, c == c_)

            @pl.when(jnp.logical_not(is_me))
            def _(e=e, c_=c_):
                yo_copy(e, c_).start()

            @pl.when(is_me)
            def _(e=e, c_=c_):
                cp = pltpu.make_async_copy(syo.at[e, c_], yo.at[h], loc.at[7])
                cp.start()
                cp.wait()

    womat = wob[...].reshape(HC, C)
    a_other = act[pl.ds(pl.multiple_of((1 - c) * A, A), A), :]
    part_s[...] = jnp.dot(a_other, womat, preferred_element_type=F32).astype(BF16)
    sent.append(send(part_s, part_r, s_misc.at[8], r_misc.at[8], partner))
    a_own = act[pl.ds(pl.multiple_of(c * A, A), A), :]
    node_own = jnp.dot(a_own, womat, preferred_element_type=F32) + fx[f_rows, :].astype(F32)

    msg_relay(0)
    msg_first(2)
    msg_relay(1)
    msg_first(3)
    msg_y(0)
    msg_relay(2)
    msg_y(1)
    msg_relay(3)
    for h_ in range(4):
        @pl.when(jnp.logical_or(h_ != h, c != half))
        def _(h_=h_):
            arrived(yo.at[h_], s_yo.at[0], r_yo.at[h_], dev(ylo, h_, x, half))

    total = yo[0].astype(F32) + yo[1].astype(F32) + yo[2].astype(F32) + yo[3].astype(F32)
    gout_o[0] = total.astype(BF16)
    gf[...] = total
    chosen = jnp.full((32, FRAG), frag[0], jnp.int32)

    def decoded(piece):
        scale = (jnp.max(jnp.abs(piece), axis=1, keepdims=True) + TINY).astype(BF16).astype(F32)
        code = (piece / scale).astype(BF16).astype(F32)
        return (scale * code).astype(BF16)

    def outer_send(m, buf, ss, rs):
        for d in range(1, 16):
            sent.append(send(tb.at[m], buf.at[r], ss.at[d], rs.at[d], ((r + d) % 16, f)))

    def outer_sum(m, buf, ss, rs):
        for d in range(1, 16):
            r_ = (r + 16 - d) % 16
            arrived(buf.at[r_], ss.at[d], rs.at[d], (r_, f))
        outer_o[m] = jnp.sum(buf[...].astype(F32), axis=0)

    piece = jnp.zeros((32, FRAG), F32)
    for b in range(C // FRAG):
        piece = jnp.where(chosen == b, gf[:, b * FRAG : (b + 1) * FRAG], piece)
    term = decoded(piece)
    tb[1] = term
    oo[r] = term
    outer_send(1, oo, s_oo, r_oo)

    msg_y(2)
    msg_y(3)
    msg_sum(0)
    term = decoded(jnp.where(chosen < 4, gm[0, 0], gm[1, 0]))
    tb[0] = term
    om[r] = term
    outer_send(0, om, s_om, r_om)
    arrived(part_r, s_misc.at[8], r_misc.at[8], partner)
    node_o[...] = (node_own + part_r[...].astype(F32)).astype(BF16)
    outer_sum(1, oo, s_oo, r_oo)
    for k in (1, 2, 3):
        msg_sum(k)
    for c_ in (0, 1):
        for k, v in enumerate(turned(32, True, lambda k: gm[c_, k])):
            gmsg_o[0, :, c_ * HC + k * FRAG : c_ * HC + (k + 1) * FRAG] = v.astype(BF16)
    outer_sum(0, om, s_om, r_om)

    for cp in sent:
        cp.wait_send()

    @pl.when(up_ok)
    def _():
        for c_ in (0, 1):
            up_copy(c_).wait_send()

    @pl.when(dn_ok)
    def _():
        for c_ in (0, 1):
            dn_copy(c_).wait_send()

    @pl.when(half != c)
    def _():
        wo_partner().wait_send()

    for n in (0, 1):
        for i in range(3):
            wm_x(n, i).wait_send()
        for i in range(3):
            for u in (0, 1):
                wm_z(n, i, u).wait_send()
    for u in (0, 1):
        wm_z(1, 3, u).wait_send()

    for parity in (0, 1):
        @pl.when(par == parity)
        def _(parity=parity):
            for j in y_of[parity]:
                for c_ in (0, 1):
                    wm_y(j, c_).wait_send()
            if parity:
                for u in (0, 1):
                    wm_z(0, 3, u).wait_send()

    @pl.when(h % 2 == par)
    def _():
        for j in range(3):
            wo_y(j).wait_send()

    @pl.when(h != 2 * c + par)
    def _():
        for u in (0, 1):
            wo_own_z(u).wait_send()
    @pl.when(q > 0)
    def _():
        rim_dn().wait_send()

    @pl.when(q < 15)
    def _():
        rim_up().wait_send()

    for e in (0, 1):
        for c_ in (0, 1):
            @pl.when(jnp.logical_not(jnp.logical_and(2 * c + e == h, c == c_)))
            def _(e=e, c_=c_):
                yo_copy(e, c_).wait_send()


def shards(feats, src, dist, ids, wm, wo, radial, cot, frag):
    vm = pl.BlockSpec(memory_space=pltpu.VMEM)
    dma = lambda *n: pltpu.SemaphoreType.DMA(n)
    V = pltpu.VMEM
    return pl.pallas_call(
        body,
        out_shape=(
            jax.ShapeDtypeStruct((A, C), BF16),
            jax.ShapeDtypeStruct((1, 32, C), BF16),
            jax.ShapeDtypeStruct((1, 32, C), BF16),
            jax.ShapeDtypeStruct((2, 32, FRAG), F32),
        ),
        in_specs=[pl.BlockSpec(memory_space=pl.ANY)] * 8 + [pl.BlockSpec(memory_space=pltpu.SMEM)],
        out_specs=(vm,) * 4,
        scratch_shapes=[
            V((4, 4, 2, 32, HC), BF16),
            V((2, 4, 2, 32, C), BF16),
            V((32, C), BF16),
            V((32, C), BF16),
            V((BASIS, C), F32),
            V((4, 4, 2, 1, A), jnp.int32),
            V((EXT, C), BF16),
            V((2, A, C), BF16),
            V((2, NB, A), jnp.int32),
            V((2, NB, A), F32),
            V((A, C), BF16),
            V((H, HC), BF16),
            V((H, HC), BF16),
            V((6, 64, C), BF16),
            V((4, 6, A, FRAG), BF16),
            V((4, 32, C), BF16),
            V((4, 4, 2, 32, FRAG), BF16),
            V((16, 32, FRAG), BF16),
            V((16, 32, FRAG), BF16),
            V((BASIS, NB, A), F32),
            V((BASIS * W, A), F32),
            V((2, W, BASIS * A), BF16),
            V((2, A, BASIS * W), BF16),
            V((BASIS * W, HC), BF16),
            V((2 * A, HC), BF16),
            V((2 * A, HC), F32),
            V((2, 4, 64, 2 * A), BF16),
            V((4, 4, 64, 2 * A), BF16),
            V((2 * A, C), BF16),
            V((BASIS * A, HC), BF16),
            V((EXT, HC), F32),
            V((2 * A, HC), BF16),
            V((A, C), BF16),
            V((2, H, HC), BF16),
            V((6, 64, C), BF16),
            V((4, 64, C), F32),
            V((4, 6, A, FRAG), BF16),
            V((4, 4, A, FRAG), F32),
            V((2, 2, 32, C), BF16),
            V((4, 4, 2, 32, FRAG), BF16),
            V((32, C), F32),
            V((2, 4, 32, FRAG), F32),
            V((2, 32, FRAG), BF16),
            dma(10),
            dma(7), dma(7), dma(7), dma(7), dma(4), dma(7),
            dma(2, 3), dma(2, 3), dma(2, 4, 2), dma(2, 4, 2), dma(3), dma(3),
            dma(4), dma(4), dma(4, 2), dma(4, 2),
            dma(9), dma(9), dma(6), dma(6), dma(4, 6), dma(4, 6),
            dma(4), dma(4), dma(4, 8), dma(4, 8), dma(16), dma(16), dma(16), dma(16),
        ],
        compiler_params=pltpu.CompilerParams(
            collective_id=0, has_side_effects=True, vmem_limit_bytes=56 << 20
        ),
        name="step",
    )(feats, src, dist, ids, wm, wo, radial, cot, frag)


def solution(mesh):
    placed = (
        P(("replica", "fsdp"), None),
        P(None, ("replica", "fsdp")),
        P(None, ("replica", "fsdp")),
        P("replica", "fsdp"),
        P("fsdp", None),
        P("fsdp", None),
        P(),
        P(("replica", "fsdp"), None),
        P(),
    )
    return jax.shard_map(
        shards,
        mesh=mesh,
        in_specs=placed,
        out_specs=(
            P(("replica", "fsdp"), None),
            P("replica", "fsdp", None),
            P("replica", "fsdp", None),
            P(None, "fsdp", None),
        ),
        check_vma=False,
    )
```

time: 89.9 us -> 78.2 us (0.87)
  the two profiles are of different devices: /device:TPU:3 before, /device:TPU:2 now
where the time goes in v2:
time: 78.2 us; the launch traced here: 77.9 us
  Pallas kernels  72.6 us (93%)
  local copies, waits for them, and re-layouts  3.94 us (5%)
  between operations  1.3 us (2%)
    pallas_call x1, Pallas kernels, shards(): pl.pallas_call(body, out_shape=(jax.ShapeDtypeStruct((A, C), BF16), jax.S...  72.6 us
    unnamed x10, local copies, waits for them, and re-layouts  3.94 us

profile of v2, /device:TPU:2, one launch (start us, length us, event | category | flops | bytes accessed | tf_op | source)
XLA Modules:
  0.0 77.9 jit_solution(16986088258724090883)
XLA Ops:
  1.3 72.6 %step.1 = (bf16[128,1024]{1,0:T(8,128)(2,1)}, bf16[1,32,1024]{2,1,0:T(8,128)(2,1)}, bf16[1,32,1024]{2,1,0:T(8,128)(2,1)}, f32[2,32,128]{2,1,0:T(8,128)}) custom-call(bf16[128,1024]{1,0:T(8,128)(2,1)} %feats.1, s32[12,128]{1,0:T(8,128)} %src.1, f32[12,128]{1,0:T(8,128)} %dist.1, s32[1,128]{1,0:T(1,128)} %ids.1, bf16[32,1024]{1,0:T(8,128)(2,1)} %wm.1, ...), custom_call_target="tpu_custom_call" | custom-call | tf_op jit(solution)/shard_map/step/pallas_call | solution.py:755
  73.9 0.0 copy-start.1
  73.9 1.7 %copy.18 = bf16[128,1024]{1,0:T(8,128)(2,1)} copy(bf16[128,1024]{1,0:T(8,128)(2,1)} %get-tuple-element.8) | data formatting | bytes 524288
  75.6 0.0 copy-done.1
  75.6 0.0 copy-start
  75.6 0.6 copy.19
  76.3 0.2 copy-done
  76.5 0.0 copy-start.2
  76.5 0.6 copy.20
  77.1 0.1 copy-done.2
  77.3 0.6 copy.21
Async XLA Ops:
  73.9 1.7 %copy-start.1 = (bf16[1,32,1024]{2,1,0:T(8,128)(2,1)S(1)}, bf16[1,32,1024]{2,1,0:T(8,128)(2,1)}, u32[]{:S(2)}) copy-start(bf16[1,32,1024]{2,1,0:T(8,128)(2,1)} %get-tuple-element.9) | copy-start | bytes 196612
  75.6 0.9 %copy-start = (bf16[1,32,1024]{2,1,0:T(8,128)(2,1)S(1)}, bf16[1,32,1024]{2,1,0:T(8,128)(2,1)}, u32[]{:S(2)}) copy-start(bf16[1,32,1024]{2,1,0:T(8,128)(2,1)} %get-tuple-element.10) | copy-start | bytes 196612
  76.5 0.8 copy-start.2

commit v3 on v2

--- a/solution.py
+++ b/solution.py
@@ -30,11 +30,11 @@
 
 def body(
     feats, src, dist, ids, wm, wo, radial_h, cot, frag,
-    node_o, gmsg_o, gout_o, outer_o,
+    node_h, gmsg_h, gout_h, outer_h,
     wmb, wob, wmv, wov, radial, idb, fx, cotb, srcb, distb, part_r,
     rim_lo, rim_hi, xo, xm, yo, ym, oo, om,
     bas, mtv, mtc, mc, ps, act, dsl, act_t, feats_t, dout, rr, spread, dproj,
-    part_s, rim_s, so, ko, sm, km, syo, sym, gf, gm, tb,
+    part_s, rim_s, so, ko, sm, km, syo, sym, gf, gm, tb, node_o, gmsg_o, gout_o, outer_o,
     loc, s_wy, r_wy, s_iy, r_iy, s_oy, r_oy, s_wx, r_wx, s_wz, r_wz, s_ix, r_ix,
     s_ox, r_ox, s_oz, r_oz,
     s_misc, r_misc, s_xo, r_xo, s_xm, r_xm, s_yo, r_yo, s_ym, r_ym, s_oo, r_oo, s_om, r_om,
@@ -74,6 +74,18 @@
         pltpu.make_async_remote_copy(
             src_ref=b_, dst_ref=b_, send_sem=ss, recv_sem=rs, device_id=frm, device_id_type=MESH
         ).wait_recv()
+
+    def put(i, a_, b_):
+        cp = pltpu.make_async_copy(a_, b_, loc.at[10 + i])
+        cp.start()
+        puts.append(cp)
+
+    puts = []
+    def both(ref, ss, rs):
+        return pltpu.make_async_remote_copy(
+            src_ref=ref, dst_ref=ref, send_sem=ss, recv_sem=rs, device_id=partner,
+            device_id_type=MESH,
+        )
 
     bar = pltpu.get_barrier_semaphore()
     greet = [partner]
@@ -131,39 +143,6 @@
     sent = []
     other = pl.ds(pl.multiple_of((1 - c) * HC, HC), HC)
     mine_c = pl.ds(pl.multiple_of(c * HC, HC), HC)
-    sent.append(send(wmv.at[:, other], wmb.at[h, x, c], s_wy.at[6], r_wy.at[6], partner))
-
-    def wm_y(j, c_):
-        yl, hh = y_to[j]
-        return pltpu.make_async_remote_copy(
-            src_ref=wmv.at[:, pl.ds(c_ * HC, HC)], dst_ref=wmb.at[h, x, c],
-            send_sem=s_wy.at[2 * j + c_], recv_sem=r_wy.at[2 * j + c],
-            device_id=dev(yl, hh, x, c_), device_id_type=MESH,
-        )
-
-    def wo_y(j):
-        yl, hh = y_to[j]
-        return pltpu.make_async_remote_copy(
-            src_ref=wov, dst_ref=wob.at[h % 2, x, c],
-            send_sem=s_oy.at[j], recv_sem=r_oy.at[2 * j + c],
-            device_id=dev(yl, hh, x, half), device_id_type=MESH,
-        )
-
-    y_of = ((2,), (0, 1))
-    for parity in (0, 1):
-        @pl.when(par == parity)
-        def _(parity=parity):
-            for j in y_of[parity]:
-                for c_ in (0, 1):
-                    wm_y(j, c_).start()
-
-    @pl.when(h % 2 == par)
-    def _():
-        for j in (2, 1, 0):
-            wo_y(j).start()
-
-    sent.append(send(srcb.at[c], srcb.at[c], s_misc.at[0], r_misc.at[0], partner))
-    sent.append(send(distb.at[c], distb.at[c], s_misc.at[1], r_misc.at[1], partner))
     my_ids = idb.at[h, x, c]
     sent.append(send(my_ids, my_ids, s_iy.at[6], r_iy.at[6], partner))
     for j, hh in enumerate((hb, ha, h2)):
@@ -173,7 +152,39 @@
                     my_ids, my_ids, s_iy.at[2 * j + c_], r_iy.at[2 * j + c], dev(ylo, hh, x, c_)
                 )
             )
-
+    sent.append(send(wmv.at[:, other], wmb.at[h, x, c], s_wy.at[6], r_wy.at[6], partner))
+
+    def wm_y(j, c_):
+        yl, hh = y_to[j]
+        return pltpu.make_async_remote_copy(
+            src_ref=wmv.at[:, pl.ds(c_ * HC, HC)], dst_ref=wmb.at[h, x, c],
+            send_sem=s_wy.at[2 * j + c_], recv_sem=r_wy.at[2 * j + c],
+            device_id=dev(yl, hh, x, c_), device_id_type=MESH,
+        )
+
+    def wo_y(j):
+        yl, hh = y_to[j]
+        return pltpu.make_async_remote_copy(
+            src_ref=wov, dst_ref=wob.at[h % 2, x, c],
+            send_sem=s_oy.at[j], recv_sem=r_oy.at[2 * j + c],
+            device_id=dev(yl, hh, x, half), device_id_type=MESH,
+        )
+
+    y_of = ((2,), (0, 1))
+    for parity in (0, 1):
+        @pl.when(par == parity)
+        def _(parity=parity):
+            for j in y_of[parity]:
+                for c_ in (0, 1):
+                    wm_y(j, c_).start()
+
+    @pl.when(h % 2 == par)
+    def _():
+        for j in (2, 1, 0):
+            wo_y(j).start()
+
+    sent.append(send(srcb.at[c], srcb.at[c], s_misc.at[0], r_misc.at[0], partner))
+    sent.append(send(distb.at[c], distb.at[c], s_misc.at[1], r_misc.at[1], partner))
     def wm_in(k):
         if k == 0:
             arrived(wmb.at[h, x, 1 - c], s_wy.at[6], r_wy.at[6], partner)
@@ -339,6 +350,7 @@
     wm_x_start(0, 1)
     wm_x_start(1, 0)
     wm_x_start(1, 1)
+    build(0, 1)
     arrived(idb.at[h, x, 1 - c], s_iy.at[6], r_iy.at[6], partner)
     for k, yb in enumerate(y_in):
         for c_ in (0, 1):
@@ -347,7 +359,6 @@
     for i, x_ in enumerate((xp, xn, x2)):
         ref = idb.at[:, x]
         sent.append(send(ref, ref, s_ix.at[i], r_ix.at[i], dev(ylo, h, x_, c)))
-    build(0, 1)
     wo_in()
     wm_x_in(0, 0)
     wm_x_in(0, 1)
@@ -442,13 +453,6 @@
     ko[2] = v[:64]
     ko[3] = v[64:]
 
-    arrived(xo.at[0], s_xo.at[0], r_xo.at[0], left)
-    so[4] = (ko[0] + xo[0].astype(F32)).astype(BF16)
-    sent.append(send(so.at[4], xo.at[4], s_xo.at[4], r_xo.at[4], right))
-    arrived(xo.at[1], s_xo.at[1], r_xo.at[1], right)
-    so[5] = (ko[1] + xo[1].astype(F32)).astype(BF16)
-    sent.append(send(so.at[5], xo.at[5], s_xo.at[5], r_xo.at[5], left))
-
     for i, x_ in enumerate((xn, xp, x2)):
         for u in (0, 1):
             arrived(wob.at[1 - par, x_, u], s_oz.at[i, u], r_oz.at[i, u], z_in[u])
@@ -497,6 +501,13 @@
     def _():
         rim_up().start()
 
+    arrived(xo.at[0], s_xo.at[0], r_xo.at[0], left)
+    so[4] = (ko[0] + xo[0].astype(F32)).astype(BF16)
+    sent.append(send(so.at[4], xo.at[4], s_xo.at[4], r_xo.at[4], right))
+    arrived(xo.at[1], s_xo.at[1], r_xo.at[1], right)
+    so[5] = (ko[1] + xo[1].astype(F32)).astype(BF16)
+    sent.append(send(so.at[5], xo.at[5], s_xo.at[5], r_xo.at[5], left))
+
     @pl.when(q > 0)
     def _():
         arrived(rim_lo, s_misc.at[7], r_misc.at[7], chip(qp, c))
@@ -549,47 +560,38 @@
 
     def msg_leg(k, i):
         to = (right, left, right, left, right, left)[i]
-        sent.append(send(sm.at[k, i], xm.at[k, i], s_xm.at[k, i], r_xm.at[k, i], to))
-
-    def msg_in(k, i):
-        frm = (left, right, left, right, left, right)[i]
-        arrived(xm.at[k, i], s_xm.at[k, i], r_xm.at[k, i], frm)
+        send(sm.at[k, i], xm.at[k, i], s_xm.at[0], r_xm.at[k, 0 if i < 2 else 1], to)
 
     def msg_first(k):
         for i in range(4):
             msg_leg(k, i)
 
     def msg_relay(k):
+        both(xm.at[k, pl.ds(0, 2)], s_xm.at[0], r_xm.at[k, 0]).wait_recv()
         for i in (0, 1):
-            msg_in(k, i)
             sm[k, 4 + i] = (km[k, i] + xm[k, i].astype(F32)).astype(BF16)
             msg_leg(k, 4 + i)
 
     def msg_y(k):
-        for i in (2, 3, 4, 5):
-            msg_in(k, i)
+        both(xm.at[k, pl.ds(2, 4)], s_xm.at[0], r_xm.at[k, 1]).wait_recv()
         lo = (km[k, 2] + xm[k, 3].astype(F32) + xm[k, 4].astype(F32)).astype(BF16)
         hi = (km[k, 3] + xm[k, 2].astype(F32) + xm[k, 5].astype(F32)).astype(BF16)
         sym[k, 0:2] = lo.reshape(2, 2, 32, FRAG)
         sym[k, 2:4] = hi.reshape(2, 2, 32, FRAG)
-        for d in range(7, 0, -1):
+        for d in (5, 4, 7, 6, 3, 2, 1):
             hh, c_ = (h + d // 2) % 4, (c + d) % 2
-            sent.append(
-                send(
-                    sym.at[k, hh, c_], ym.at[k, h, c], s_ym.at[k, d], r_ym.at[k, d],
-                    dev(ylo, hh, x, c_),
-                )
+            send(
+                sym.at[k, hh, c_], ym.at[k, 2 * h + c], s_ym.at[k], r_ym.at[k],
+                dev(ylo, hh, x, c_),
             )
-        ym[k, h, c] = sym[k, h, c]
+        ym[k, 2 * h + c] = sym[k, h, c]
 
     def msg_sum(k):
-        for d in range(1, 8):
-            hh, c_ = (h + 4 - d // 2) % 4, (c + d) % 2
-            arrived(ym.at[k, hh, c_], s_ym.at[k, d], r_ym.at[k, d], dev(ylo, hh, x, c_))
+        both(ym.at[k, pl.ds(0, 7)], s_ym.at[k], r_ym.at[k]).wait_recv()
         for c_ in (0, 1):
             gm[c_, k] = (
-                ym[k, 0, c_].astype(F32) + ym[k, 1, c_].astype(F32)
-                + ym[k, 2, c_].astype(F32) + ym[k, 3, c_].astype(F32)
+                ym[k, c_].astype(F32) + ym[k, 2 + c_].astype(F32)
+                + ym[k, 4 + c_].astype(F32) + ym[k, 6 + c_].astype(F32)
             )
 
     msg_first(0)
@@ -645,6 +647,7 @@
 
     total = yo[0].astype(F32) + yo[1].astype(F32) + yo[2].astype(F32) + yo[3].astype(F32)
     gout_o[0] = total.astype(BF16)
+    put(2, gout_o, gout_h)
     gf[...] = total
     chosen = jnp.full((32, FRAG), frag[0], jnp.int32)
 
@@ -653,14 +656,18 @@
         code = (piece / scale).astype(BF16).astype(F32)
         return (scale * code).astype(BF16)
 
+    peers = sorted(
+        ((dy, dz) for dy in range(2) for dz in range(8) if dy or dz),
+        key=lambda p_: -(p_[0] + min(p_[1], 8 - p_[1])),
+    )
+
     def outer_send(m, buf, ss, rs):
-        for d in range(1, 16):
-            sent.append(send(tb.at[m], buf.at[r], ss.at[d], rs.at[d], ((r + d) % 16, f)))
+        for dy, dz in peers:
+            to = ((ylo + dy) % 2 * 8 + (z + dz) % 8, f)
+            send(tb.at[m], buf.at[r], ss.at[0], rs.at[0], to)
 
     def outer_sum(m, buf, ss, rs):
-        for d in range(1, 16):
-            r_ = (r + 16 - d) % 16
-            arrived(buf.at[r_], ss.at[d], rs.at[d], (r_, f))
+        both(buf.at[pl.ds(0, 15)], ss.at[0], rs.at[0]).wait_recv()
         outer_o[m] = jnp.sum(buf[...].astype(F32), axis=0)
 
     piece = jnp.zeros((32, FRAG), F32)
@@ -680,14 +687,24 @@
     outer_send(0, om, s_om, r_om)
     arrived(part_r, s_misc.at[8], r_misc.at[8], partner)
     node_o[...] = (node_own + part_r[...].astype(F32)).astype(BF16)
+    put(0, node_o, node_h)
     outer_sum(1, oo, s_oo, r_oo)
     for k in (1, 2, 3):
         msg_sum(k)
     for c_ in (0, 1):
         for k, v in enumerate(turned(32, True, lambda k: gm[c_, k])):
             gmsg_o[0, :, c_ * HC + k * FRAG : c_ * HC + (k + 1) * FRAG] = v.astype(BF16)
+    put(1, gmsg_o, gmsg_h)
     outer_sum(0, om, s_om, r_om)
-
+    put(3, outer_o, outer_h)
+
+    for cp in puts:
+        cp.wait()
+    both(sm, s_xm.at[0], s_xm.at[0]).wait_send()
+    for k in range(4):
+        both(ym.at[k, pl.ds(0, 7)], s_ym.at[k], r_ym.at[k]).wait_send()
+    both(oo.at[pl.ds(0, 15)], s_oo.at[0], r_oo.at[0]).wait_send()
+    both(om.at[pl.ds(0, 15)], s_om.at[0], r_om.at[0]).wait_send()
     for cp in sent:
         cp.wait_send()
 
@@ -748,11 +765,20 @@
                 yo_copy(e, c_).wait_send()
 
 
+def finish(*refs):
+    sems = refs[8]
+    copies = [pltpu.make_async_copy(refs[i], refs[4 + i], sems.at[i]) for i in range(4)]
+    for cp in copies:
+        cp.start()
+    for cp in copies:
+        cp.wait()
+
+
 def shards(feats, src, dist, ids, wm, wo, radial, cot, frag):
     vm = pl.BlockSpec(memory_space=pltpu.VMEM)
     dma = lambda *n: pltpu.SemaphoreType.DMA(n)
     V = pltpu.VMEM
-    return pl.pallas_call(
+    results = pl.pallas_call(
         body,
         out_shape=(
             jax.ShapeDtypeStruct((A, C), BF16),
@@ -761,7 +787,7 @@
             jax.ShapeDtypeStruct((2, 32, FRAG), F32),
         ),
         in_specs=[pl.BlockSpec(memory_space=pl.ANY)] * 8 + [pl.BlockSpec(memory_space=pltpu.SMEM)],
-        out_specs=(vm,) * 4,
+        out_specs=(pl.BlockSpec(memory_space=pl.ANY),) * 4,
         scratch_shapes=[
             V((4, 4, 2, 32, HC), BF16),
             V((2, 4, 2, 32, C), BF16),
@@ -779,7 +805,7 @@
             V((6, 64, C), BF16),
             V((4, 6, A, FRAG), BF16),
             V((4, 32, C), BF16),
-            V((4, 4, 2, 32, FRAG), BF16),
+            V((4, 8, 32, FRAG), BF16),
             V((16, 32, FRAG), BF16),
             V((16, 32, FRAG), BF16),
             V((BASIS, NB, A), F32),
@@ -806,18 +832,32 @@
             V((32, C), F32),
             V((2, 4, 32, FRAG), F32),
             V((2, 32, FRAG), BF16),
-            dma(10),
+            V((A, C), BF16),
+            V((1, 32, C), BF16),
+            V((1, 32, C), BF16),
+            V((2, 32, FRAG), F32),
+            dma(14),
             dma(7), dma(7), dma(7), dma(7), dma(4), dma(7),
             dma(2, 3), dma(2, 3), dma(2, 4, 2), dma(2, 4, 2), dma(3), dma(3),
             dma(4), dma(4), dma(4, 2), dma(4, 2),
-            dma(9), dma(9), dma(6), dma(6), dma(4, 6), dma(4, 6),
-            dma(4), dma(4), dma(4, 8), dma(4, 8), dma(16), dma(16), dma(16), dma(16),
+            dma(9), dma(9), dma(6), dma(6), dma(1), dma(4, 2),
+            dma(4), dma(4), dma(4), dma(4), dma(1), dma(1), dma(1), dma(1),
         ],
         compiler_params=pltpu.CompilerParams(
             collective_id=0, has_side_effects=True, vmem_limit_bytes=56 << 20
         ),
         name="step",
     )(feats, src, dist, ids, wm, wo, radial, cot, frag)
+    anywhere = pl.BlockSpec(memory_space=pl.ANY)
+    return pl.pallas_call(
+        finish,
+        out_shape=tuple(jax.ShapeDtypeStruct(v.shape, v.dtype) for v in results),
+        in_specs=[vm] * 4,
+        out_specs=(anywhere,) * 4,
+        scratch_shapes=[dma(4)],
+        compiler_params=pltpu.CompilerParams(vmem_limit_bytes=60 << 20),
+        name="finish",
+    )(*results)
 
 
 def solution(mesh):

time: 78.2 us -> 74.1 us (0.948)
  the two profiles are of different devices: /device:TPU:2 before, /device:TPU:23 now
where the time goes in v3:
time: 74.1 us; the launch traced here: 73.9 us
  Pallas kernels  72.6 us (98%)
  between operations  1.29 us (2%)
    pallas_call x1, Pallas kernels, shards(): pl.pallas_call(body, out_shape=(jax.ShapeDtypeStruct((A, C), BF16), jax.S...  70.9 us
    pallas_call x1, Pallas kernels, shards(): pl.pallas_call(finish, out_shape=tuple((jax.ShapeDtypeStruct(v.shape, v.d...  1.77 us

profile of v3, /device:TPU:23, one launch (start us, length us, event | category | flops | bytes accessed | tf_op | source)
XLA Modules:
  0.0 73.9 jit_solution(12949165635713632709)
XLA Ops:
  1.3 70.9 %step.1 = (bf16[128,1024]{1,0:T(8,128)(2,1)}, bf16[1,32,1024]{2,1,0:T(8,128)(2,1)}, bf16[1,32,1024]{2,1,0:T(8,128)(2,1)}, f32[2,32,128]{2,1,0:T(8,128)}) custom-call(bf16[128,1024]{1,0:T(8,128)(2,1)} %feats.1, s32[12,128]{1,0:T(8,128)} %src.1, f32[12,128]{1,0:T(8,128)} %dist.1, s32[1,128]{1,0:T(1,128)} %ids.1, bf16[32,1024]{1,0:T(8,128)(2,1)} %wm.1, ...), custom_call_target="tpu_custom_call" | custom-call | tf_op jit(solution)/shard_map/step/pallas_call | solution.py:781
  72.2 1.8 %finish.1 = (bf16[128,1024]{1,0:T(8,128)(2,1)}, bf16[1,32,1024]{2,1,0:T(8,128)(2,1)}, bf16[1,32,1024]{2,1,0:T(8,128)(2,1)}, f32[2,32,128]{2,1,0:T(8,128)}) custom-call(bf16[128,1024]{1,0:T(8,128)(2,1)} %get-tuple-element.8.refs_0_, bf16[1,32,1024]{2,1,0:T(8,128)(2,1)} %get-tuple-element.9.refs_1_, bf16[1,32,1024]{2,1,0:T(8,128)(2,1)} %get-tuple-element.10.refs_2_, ...), custom_call_target="tpu_custom_call" | custom-call | tf_op jit(solution)/shard_map/finish/pallas_call | solution.py:852

commit v4 on v3

--- a/solution.py
+++ b/solution.py
@@ -205,14 +205,14 @@
     def wm_x(n, i):
         ref = wmb.at[taken[n], x]
         return pltpu.make_async_remote_copy(
-            src_ref=ref, dst_ref=ref, send_sem=s_wx.at[n, i], recv_sem=r_wx.at[n, i],
+            src_ref=ref, dst_ref=ref, send_sem=s_wx.at[n], recv_sem=r_wx.at[n, i],
             device_id=(right, left, far)[i], device_id_type=MESH,
         )
 
     def wm_z(n, i, u):
         ref = wmb.at[taken[n], (xn, xp, x2, x)[i], u]
         return pltpu.make_async_remote_copy(
-            src_ref=ref, dst_ref=ref, send_sem=s_wz.at[n, i, u], recv_sem=r_wz.at[n, i, u],
+            src_ref=ref, dst_ref=ref, send_sem=s_wz.at[n], recv_sem=r_wz.at[n],
             device_id=z_to[u], device_id_type=MESH,
         )
 
@@ -229,7 +229,7 @@
 
     def wm_x_in(n, i):
         ref = wmb.at[taken[n], (xn, xp, x2)[i]]
-        arrived(ref, s_wx.at[n, i], r_wx.at[n, i], (left, right, far)[i])
+        arrived(ref, s_wx.at[n], r_wx.at[n, i], (left, right, far)[i])
         for u in (0, 1):
             wm_z(n, i, u).start()
 
@@ -327,7 +327,7 @@
     def wo_own_z(u):
         ref = wob.at[par, x, u]
         return pltpu.make_async_remote_copy(
-            src_ref=ref, dst_ref=ref, send_sem=s_oz.at[3, u], recv_sem=r_oz.at[3, u],
+            src_ref=ref, dst_ref=ref, send_sem=s_oz.at[0], recv_sem=r_oz.at[0],
             device_id=z_to[u], device_id_type=MESH,
         )
 
@@ -342,7 +342,7 @@
         arrived(wob.at[par, col], s_ox.at[i], r_ox.at[i], (left, right, far)[i])
         for u in (0, 1):
             ref = wob.at[par, col, u]
-            sent.append(send(ref, ref, s_oz.at[i, u], r_oz.at[i, u], z_to[u]))
+            send(ref, ref, s_oz.at[0], r_oz.at[0], z_to[u])
 
     arrived(srcb.at[1 - c], s_misc.at[0], r_misc.at[0], partner)
     arrived(distb.at[1 - c], s_misc.at[1], r_misc.at[1], partner)
@@ -358,10 +358,10 @@
             arrived(idb.at[yb, x, c_], s_iy.at[i], r_iy.at[i], dev(ylo, yb, x, c_))
     for i, x_ in enumerate((xp, xn, x2)):
         ref = idb.at[:, x]
-        sent.append(send(ref, ref, s_ix.at[i], r_ix.at[i], dev(ylo, h, x_, c)))
-    wo_in()
+        send(ref, ref, s_ix.at[0], r_ix.at[0], dev(ylo, h, x_, c))
     wm_x_in(0, 0)
     wm_x_in(0, 1)
+    wo_in()
     build(1, 0)
     wm_x_in(0, 2)
     wm_x_in(1, 1)
@@ -386,8 +386,7 @@
     wo_z()
     wo_x_in(0)
     wo_x_in(1)
-    for i, x_ in enumerate((xn, xp, x2)):
-        arrived(idb.at[:, x_], s_ix.at[i], r_ix.at[i], dev(ylo, h, x_, c))
+    both(idb.at[pl.ds(0, 3)], s_ix.at[0], r_ix.at[0]).wait_recv()
     all_ids = idb[...].reshape(32, A)
     for p in (0, 1):
         mine = idb[h, x, p]
@@ -401,18 +400,12 @@
             cols = slice(t * A, (t + 1) * A)
             dout[p * A : (p + 1) * A, cols] = (cotb[p, :, cols].astype(F32) * wcol).astype(BF16)
 
-    for n in (0, 1):
-        for i, col in enumerate((xn, xp, x2)):
-            for u in (0, 1):
-                arrived(wmb.at[rest[n], col, u], s_wz.at[n, i, u], r_wz.at[n, i, u], z_in[u])
-        if n:
-            for u in (0, 1):
-                arrived(wmb.at[rest[n], x, u], s_wz.at[n, 3, u], r_wz.at[n, 3, u], z_in[u])
-        else:
-            @pl.when(par == 0)
-            def _():
-                for u in (0, 1):
-                    arrived(wmb.at[rest[0], x, u], s_wz.at[0, 3, u], r_wz.at[0, 3, u], z_in[u])
+    both(wmb.at[0], s_wz.at[1], r_wz.at[1]).wait_recv()
+    for parity in (0, 1):
+        @pl.when(par == parity)
+        def _(parity=parity):
+            ref = wmb.at[0, pl.ds(0, 3)] if parity else wmb.at[0]
+            both(ref, s_wz.at[0], r_wz.at[0]).wait_recv()
 
     wmat = wmb[...].reshape(C, HC)
     proj = jnp.dot(fx[...], wmat, preferred_element_type=F32).astype(BF16)
@@ -453,14 +446,13 @@
     ko[2] = v[:64]
     ko[3] = v[64:]
 
-    for i, x_ in enumerate((xn, xp, x2)):
-        for u in (0, 1):
-            arrived(wob.at[1 - par, x_, u], s_oz.at[i, u], r_oz.at[i, u], z_in[u])
-
     @pl.when(h != 2 * c + 1 - par)
     def _():
-        for u in (0, 1):
-            arrived(wob.at[1 - par, x, u], s_oz.at[3, u], r_oz.at[3, u], z_in[u])
+        both(wob.at[0], s_oz.at[0], r_oz.at[0]).wait_recv()
+
+    @pl.when(h == 2 * c + 1 - par)
+    def _():
+        both(wob.at[0, pl.ds(0, 3)], s_oz.at[0], r_oz.at[0]).wait_recv()
 
     @pl.when(h == 2 * c + 1 - par)
     def _():
@@ -625,21 +617,20 @@
                 cp.start()
                 cp.wait()
 
+    msg_relay(0)
+    msg_first(2)
     womat = wob[...].reshape(HC, C)
     a_other = act[pl.ds(pl.multiple_of((1 - c) * A, A), A), :]
     part_s[...] = jnp.dot(a_other, womat, preferred_element_type=F32).astype(BF16)
     sent.append(send(part_s, part_r, s_misc.at[8], r_misc.at[8], partner))
     a_own = act[pl.ds(pl.multiple_of(c * A, A), A), :]
     node_own = jnp.dot(a_own, womat, preferred_element_type=F32) + fx[f_rows, :].astype(F32)
-
-    msg_relay(0)
-    msg_first(2)
     msg_relay(1)
     msg_first(3)
+    msg_relay(2)
     msg_y(0)
-    msg_relay(2)
+    msg_relay(3)
     msg_y(1)
-    msg_relay(3)
     for h_ in range(4):
         @pl.when(jnp.logical_or(h_ != h, c != half))
         def _(h_=h_):
@@ -701,6 +692,7 @@
     for cp in puts:
         cp.wait()
     both(sm, s_xm.at[0], s_xm.at[0]).wait_send()
+    both(idb.at[pl.ds(0, 3)], s_ix.at[0], r_ix.at[0]).wait_send()
     for k in range(4):
         both(ym.at[k, pl.ds(0, 7)], s_ym.at[k], r_ym.at[k]).wait_send()
     both(oo.at[pl.ds(0, 15)], s_oo.at[0], r_oo.at[0]).wait_send()
@@ -723,13 +715,8 @@
         wo_partner().wait_send()
 
     for n in (0, 1):
-        for i in range(3):
-            wm_x(n, i).wait_send()
-        for i in range(3):
-            for u in (0, 1):
-                wm_z(n, i, u).wait_send()
-    for u in (0, 1):
-        wm_z(1, 3, u).wait_send()
+        both(wmb.at[0, pl.ds(0, 3)], s_wx.at[n], s_wx.at[n]).wait_send()
+    both(wmb.at[0], s_wz.at[1], r_wz.at[1]).wait_send()
 
     for parity in (0, 1):
         @pl.when(par == parity)
@@ -737,9 +724,8 @@
             for j in y_of[parity]:
                 for c_ in (0, 1):
                     wm_y(j, c_).wait_send()
-            if parity:
-                for u in (0, 1):
-                    wm_z(0, 3, u).wait_send()
+            ref = wmb.at[0] if parity else wmb.at[0, pl.ds(0, 3)]
+            both(ref, s_wz.at[0], r_wz.at[0]).wait_send()
 
     @pl.when(h % 2 == par)
     def _():
@@ -748,8 +734,11 @@
 
     @pl.when(h != 2 * c + par)
     def _():
-        for u in (0, 1):
-            wo_own_z(u).wait_send()
+        both(wob.at[0], s_oz.at[0], r_oz.at[0]).wait_send()
+
+    @pl.when(h == 2 * c + par)
+    def _():
+        both(wob.at[0, pl.ds(0, 3)], s_oz.at[0], r_oz.at[0]).wait_send()
     @pl.when(q > 0)
     def _():
         rim_dn().wait_send()
@@ -838,8 +827,8 @@
             V((2, 32, FRAG), F32),
             dma(14),
             dma(7), dma(7), dma(7), dma(7), dma(4), dma(7),
-            dma(2, 3), dma(2, 3), dma(2, 4, 2), dma(2, 4, 2), dma(3), dma(3),
-            dma(4), dma(4), dma(4, 2), dma(4, 2),
+            dma(2), dma(2, 3), dma(2), dma(2), dma(1), dma(1),
+            dma(4), dma(4), dma(1), dma(1),
             dma(9), dma(9), dma(6), dma(6), dma(1), dma(4, 2),
             dma(4), dma(4), dma(4), dma(4), dma(1), dma(1), dma(1), dma(1),
         ],

time: 74.1 us -> 73.7 us (level)
  the two profiles are of different devices: /device:TPU:23 before, /device:TPU:31 now
where the time goes in v4:
time: 73.7 us; the launch traced here: 73.5 us
  Pallas kernels  72.2 us (98%)
  between operations  1.29 us (2%)
    pallas_call x1, Pallas kernels, shards(): pl.pallas_call(body, out_shape=(jax.ShapeDtypeStruct((A, C), BF16), jax.S...  70.5 us
    pallas_call x1, Pallas kernels, shards(): pl.pallas_call(finish, out_shape=tuple((jax.ShapeDtypeStruct(v.shape, v.d...  1.77 us

profile of v4, /device:TPU:31, one launch (start us, length us, event | category | flops | bytes accessed | tf_op | source)
XLA Modules:
  0.0 73.5 jit_solution(4228840662425191007)
XLA Ops:
  1.3 70.5 %step.1 = (bf16[128,1024]{1,0:T(8,128)(2,1)}, bf16[1,32,1024]{2,1,0:T(8,128)(2,1)}, bf16[1,32,1024]{2,1,0:T(8,128)(2,1)}, f32[2,32,128]{2,1,0:T(8,128)}) custom-call(bf16[128,1024]{1,0:T(8,128)(2,1)} %feats.1, s32[12,128]{1,0:T(8,128)} %src.1, f32[12,128]{1,0:T(8,128)} %dist.1, s32[1,128]{1,0:T(1,128)} %ids.1, bf16[32,1024]{1,0:T(8,128)(2,1)} %wm.1, ...), custom_call_target="tpu_custom_call" | custom-call | tf_op jit(solution)/shard_map/step/pallas_call | solution.py:770
  71.8 1.8 %finish.1 = (bf16[128,1024]{1,0:T(8,128)(2,1)}, bf16[1,32,1024]{2,1,0:T(8,128)(2,1)}, bf16[1,32,1024]{2,1,0:T(8,128)(2,1)}, f32[2,32,128]{2,1,0:T(8,128)}) custom-call(bf16[128,1024]{1,0:T(8,128)(2,1)} %get-tuple-element.8.refs_0_, bf16[1,32,1024]{2,1,0:T(8,128)(2,1)} %get-tuple-element.9.refs_1_, bf16[1,32,1024]{2,1,0:T(8,128)(2,1)} %get-tuple-element.10.refs_2_, ...), custom_call_target="tpu_custom_call" | custom-call | tf_op jit(solution)/shard_map/finish/pallas_call | solution.py:841

commit v5 on v4

--- a/solution.py
+++ b/solution.py
@@ -367,6 +367,7 @@
     wm_x_in(1, 1)
     wm_x_in(1, 0)
     wm_x_in(1, 2)
+    wo_z()
     build(1, 1)
     arrived(fx.at[f_other], s_misc.at[2], r_misc.at[2], partner)
     for p in (0, 1):
@@ -383,9 +384,6 @@
     def _():
         arrived(fx.at[pl.ds(H + 2 * A, H)], s_misc.at[4], r_misc.at[5], chip(qn, 0))
 
-    wo_z()
-    wo_x_in(0)
-    wo_x_in(1)
     both(idb.at[pl.ds(0, 3)], s_ix.at[0], r_ix.at[0]).wait_recv()
     all_ids = idb[...].reshape(32, A)
     for p in (0, 1):
@@ -400,6 +398,8 @@
             cols = slice(t * A, (t + 1) * A)
             dout[p * A : (p + 1) * A, cols] = (cotb[p, :, cols].astype(F32) * wcol).astype(BF16)
 
+    wo_x_in(0)
+    wo_x_in(1)
     both(wmb.at[0], s_wz.at[1], r_wz.at[1]).wait_recv()
     for parity in (0, 1):
         @pl.when(par == parity)

time: 73.7 us -> 73.7 us (level)
  the two profiles are of different devices: /device:TPU:31 before, /device:TPU:23 now
where the time goes in v5:
time: 73.7 us; the launch traced here: 73.5 us
  Pallas kernels  72.2 us (98%)
  between operations  1.29 us (2%)
    pallas_call x1, Pallas kernels, shards(): pl.pallas_call(body, out_shape=(jax.ShapeDtypeStruct((A, C), BF16), jax.S...  70.4 us
    pallas_call x1, Pallas kernels, shards(): pl.pallas_call(finish, out_shape=tuple((jax.ShapeDtypeStruct(v.shape, v.d...  1.77 us

profile of v5, /device:TPU:23, one launch (start us, length us, event | category | flops | bytes accessed | tf_op | source)
XLA Modules:
  0.0 73.5 jit_solution(14964608025583250558)
XLA Ops:
  1.3 70.4 %step.1 = (bf16[128,1024]{1,0:T(8,128)(2,1)}, bf16[1,32,1024]{2,1,0:T(8,128)(2,1)}, bf16[1,32,1024]{2,1,0:T(8,128)(2,1)}, f32[2,32,128]{2,1,0:T(8,128)}) custom-call(bf16[128,1024]{1,0:T(8,128)(2,1)} %feats.1, s32[12,128]{1,0:T(8,128)} %src.1, f32[12,128]{1,0:T(8,128)} %dist.1, s32[1,128]{1,0:T(1,128)} %ids.1, bf16[32,1024]{1,0:T(8,128)(2,1)} %wm.1, ...), custom_call_target="tpu_custom_call" | custom-call | tf_op jit(solution)/shard_map/step/pallas_call | solution.py:770
  71.7 1.8 %finish.1 = (bf16[128,1024]{1,0:T(8,128)(2,1)}, bf16[1,32,1024]{2,1,0:T(8,128)(2,1)}, bf16[1,32,1024]{2,1,0:T(8,128)(2,1)}, f32[2,32,128]{2,1,0:T(8,128)}) custom-call(bf16[128,1024]{1,0:T(8,128)(2,1)} %get-tuple-element.8.refs_0_, bf16[1,32,1024]{2,1,0:T(8,128)(2,1)} %get-tuple-element.9.refs_1_, bf16[1,32,1024]{2,1,0:T(8,128)(2,1)} %get-tuple-element.10.refs_2_, ...), custom_call_target="tpu_custom_call" | custom-call | tf_op jit(solution)/shard_map/finish/pallas_call | solution.py:841
